TPU v7x, 512 devices: a whole 4x8x8 slice. The times are simulated.
512 devices in a mesh: gx: 32 (over x_hi, z, core), gy: 8 (over y), gz: 2 (over x_lo).
Axes of the slice: x: 4 (x_hi: 2, x_lo: 2; x = x_hi * 2 + x_lo), y: 8, z: 8, core: 2. Of those that a mesh axis runs over, the one named last changes fastest.
Arguments:
- fields: float32 [2, 4, 3, 16, 512, 1024], P(None, None, None, 'gz', 'gx', 'gy'), may hold values from -6 to 6
- material: int32 [16, 512, 1024], P('gz', 'gx', 'gy'), may hold values from 0 to 3
- pml_width: int32 [6], replicated, may hold values from 2 to 4
- eps_real: float32 [4], replicated, may hold values from 1 to 12
- eps_loss: float32 [4], replicated, may hold values from 0.05 to 1
- coeffs: float32 [2, 4, 4], replicated, may hold values from -3 to 3
- ritz: float32 [2, 4], replicated, may hold values from -4 to 4
Outputs:
- basis_new: float32 [2, 4, 3, 16, 512, 1024], P(None, None, None, 'gz', 'gx', 'gy')
- residual: float32 [2, 4, 3, 16, 512, 1024], P(None, None, None, 'gz', 'gx', 'gy')
- gram_out: float32 [2, 4, 4], replicated
All inputs are finite; a program needn't handle non-finite values.
Results may differ from a plain program's by a relative error of at most 0.000078.
Values sent between devices are 32-bit elements; how exact they have to be, the bound alone decides.
A program may use at most 64 MiB of HBM per device.

v0:
```python
import functools

import jax
import jax.numpy as jnp
from jax import lax
from jax.sharding import Mesh
from jax.sharding import PartitionSpec as P

GX = ("gx_0", "gx_1", "gx_2")
GX_GY_GZ = ("gx_0", "gx_1", "gx_2", "gy", "gz")


OMEGA_SQ = 0.36
SIGMA_TOP = 3.0


def passed_along(value, axis, steps):
    count = lax.axis_size(axis)
    leading, last = (max(0, -steps), min(count, count - steps))
    return lax.ppermute(value, axis, [(source, source + steps) for source in range(leading, last)])


def one_axis_at_a_time(shard, axes):
    return functools.reduce(lax.psum, axes, shard)


def inverse_stretch(places, length, low_width, high_width):
    low_width = low_width.astype(jnp.float32)
    high_width = high_width.astype(jnp.float32)
    inside_depth = jnp.clip((low_width - places) / low_width, 0.0, 1.0) + jnp.clip(
        (places + 1.0 - length + high_width) / high_width, 0.0, 1.0
    )
    absorb = SIGMA_TOP * inside_depth * inside_depth
    scaled = 1.0 / (1.0 + absorb * absorb)
    return jnp.stack([scaled, -absorb * scaled])


def complex_mul(factor, values):
    real_part = factor[0] * values[0] - factor[1] * values[1]
    imag_part = factor[0] * values[1] + factor[1] * values[0]
    return jnp.stack([real_part, imag_part])


def spread(factor, direction, rank):
    layout = [2] + [1] * (rank - 1)
    layout[rank - 3 + direction] = factor.shape[1]
    return factor.reshape(layout)


def curl_of(components, derivative):
    return [
        derivative(components[2], 2) - derivative(components[1], 0),
        derivative(components[0], 0) - derivative(components[2], 1),
        derivative(components[1], 1) - derivative(components[0], 2),
    ]


def one_sided_curl(extended, stretches, counts):

    def derivative(number, direction):
        values = extended[direction][:, :, number]
        where_dim = 2 + direction
        ahead = lax.slice_in_dim(values, 1, counts[direction] + 1, axis=where_dim)
        behind = lax.slice_in_dim(values, 0, counts[direction], axis=where_dim)
        return complex_mul(spread(stretches[direction], direction, 5), ahead - behind)

    return curl_of([0, 1, 2], derivative)


def product(left, right):
    return jnp.einsum("am,bm->ab", left, right, precision=lax.Precision.HIGHEST)


def bilinear(values, images):
    gram_re = product(values[0], images[0]) - product(values[1], images[1])
    gram_im = product(values[0], images[1]) + product(values[1], images[0])
    return (gram_re, gram_im)


def matmul_complex(left, right):
    high = lax.Precision.HIGHEST
    real_part = jnp.matmul(left[0], right[0], precision=high) - jnp.matmul(
        left[1], right[1], precision=high
    )
    imag_part = jnp.matmul(left[0], right[1], precision=high) + jnp.matmul(
        left[1], right[0], precision=high
    )
    return jnp.stack([real_part, imag_part])


def rotate_small(gram_full, coeffs):
    turned = jnp.stack([coeffs[0].T, coeffs[1].T])
    return matmul_complex(turned, matmul_complex(gram_full, coeffs))


def rotate(values, coeffs):
    high = lax.Precision.HIGHEST
    real_part = jnp.einsum("ab,am->bm", coeffs[0], values[0], precision=high) - jnp.einsum(
        "ab,am->bm", coeffs[1], values[1], precision=high
    )
    imag_part = jnp.einsum("ab,am->bm", coeffs[0], values[1], precision=high) + jnp.einsum(
        "ab,am->bm", coeffs[1], values[0], precision=high
    )
    return jnp.stack([real_part, imag_part])


def body(fields, material, pml_width, eps_real, eps_loss, coeffs, ritz):
    counts = (fields.shape[3], fields.shape[4], fields.shape[5])
    bounds = ((4, 5), (0, 1), (2, 3))
    starts = [
        lax.axis_index("gz") * counts[0],
        lax.axis_index(GX) * counts[1],
        lax.axis_index("gy") * counts[2],
    ]
    totals = [
        counts[0] * lax.axis_size("gz"),
        counts[1] * lax.axis_size(GX),
        counts[2] * lax.axis_size("gy"),
    ]
    stretch_e = []
    for direction in range(3):
        low_slot, high_slot = bounds[direction]
        places = (starts[direction] + jnp.arange(counts[direction], dtype=jnp.int32)).astype(
            jnp.float32
        )
        stretch_e.append(
            inverse_stretch(
                places, jnp.float32(totals[direction]), pml_width[low_slot], pml_width[high_slot]
            )
        )
    eps_re = jnp.zeros(material.shape, jnp.float32)
    eps_im = jnp.zeros(material.shape, jnp.float32)
    for number in range(eps_real.shape[0]):
        chosen = (material == number).astype(jnp.float32)
        eps_re = eps_re + eps_real[number] * chosen
        eps_im = eps_im + eps_loss[number] * chosen
    eps_cell = jnp.stack([eps_re, eps_im])[:, None]
    stretch_h = []
    for direction in range(3):
        low_slot, high_slot = bounds[direction]
        places = (starts[direction] + jnp.arange(counts[direction], dtype=jnp.int32)).astype(
            jnp.float32
        ) + 0.5
        stretch_h.append(
            inverse_stretch(
                places, jnp.float32(totals[direction]), pml_width[low_slot], pml_width[high_slot]
            )
        )
    upper_z = passed_along(lax.slice_in_dim(fields, 0, 1, axis=3), "gz", -1)
    upper_x = passed_along(lax.slice_in_dim(fields, 0, 1, axis=4), GX, -1)
    upper_y = passed_along(lax.slice_in_dim(fields, 0, 1, axis=5), "gy", -1)
    field_ext = [
        jnp.concatenate([fields, rim], axis=3 + direction)
        for direction, rim in enumerate((upper_z, upper_x, upper_y))
    ]
    magnetic = jnp.stack(one_sided_curl(field_ext, stretch_h, counts), axis=2)
    lower_z = passed_along(lax.slice_in_dim(magnetic, counts[0] - 1, counts[0], axis=3), "gz", 1)
    lower_x = passed_along(lax.slice_in_dim(magnetic, counts[1] - 1, counts[1], axis=4), GX, 1)
    lower_y = passed_along(lax.slice_in_dim(magnetic, counts[2] - 1, counts[2], axis=5), "gy", 1)
    magnetic_ext = [
        jnp.concatenate([rim, magnetic], axis=3 + direction)
        for direction, rim in enumerate((lower_z, lower_x, lower_y))
    ]
    electric = one_sided_curl(magnetic_ext, stretch_e, counts)
    images = jnp.stack(
        [
            electric[number] - OMEGA_SQ * complex_mul(eps_cell, fields[:, :, number])
            for number in range(3)
        ],
        axis=2,
    )
    vectors = fields.shape[1]
    values = fields.reshape(2, vectors, -1)
    image_flat = images.reshape(2, vectors, -1)
    weight_scale = 1.0 / (3.0 * totals[0] * totals[1] * totals[2])
    local_re, local_im = bilinear(values, image_flat)
    summed_re, summed_im = (
        one_axis_at_a_time(local_re, GX_GY_GZ),
        one_axis_at_a_time(local_im, GX_GY_GZ),
    )
    gram_out = rotate_small(jnp.stack([summed_re, summed_im]), coeffs) * weight_scale
    basis_new = rotate(values, coeffs)
    rotated_image = rotate(image_flat, coeffs)
    residual = rotated_image - complex_mul(ritz[:, :, None], basis_new)
    return (basis_new.reshape(fields.shape), residual.reshape(fields.shape), gram_out)


def solution(mesh):
    split = Mesh(
        mesh.devices.reshape(2, 8, 2, mesh.shape["gy"], mesh.shape["gz"]),
        ("gx_0", "gx_1", "gx_2", "gy", "gz"),
    )
    placed = (P(None, None, None, "gz", GX, "gy"), P("gz", GX, "gy"), P(), P(), P(), P(), P())
    return jax.shard_map(
        body,
        mesh=split,
        in_specs=placed,
        out_specs=(P(None, None, None, "gz", GX, "gy"), P(None, None, None, "gz", GX, "gy"), P()),
        check_vma=False,
    )
```

profile of v0, /device:TPU:4, one launch (start us, length us, event | category | flops | bytes accessed | tf_op | source)
XLA Modules:
  0.0 173.5 jit_solution(7405450841654843532)
XLA Ops:
  0.6 4.7 %constant_dynamic-update-slice_fusion.1 = (f32[2,4,3,9,16,128]{5,1,4,3,0,2:T(4,128)}, f32[2,4,3,8,17,128]{5,1,4,3,0,2:T(4,128)}, f32[2,4,3,8,16,128]{5,1,4,3,0,2:T(4,128)S(1)}) fusion(f32[2,4,3,8,16,128]{5,4,3,2,1,0:T(8,128)} %param.7), kind=kLoop, calls=%fused_computation.122 | loop fusion | bytes 6291456
  5.3 0.7 slice.548
  6.0 10.3 %collective-permute-start.2 = (f32[2,4,3,8,1,128]{5,1,4,3,0,2:T(4,128)}, f32[2,4,3,8,1,128]{5,1,4,3,0,2:T(4,128)}, u32[]{:S(2)}, u32[]{:S(2)}) collective-permute-start(f32[2,4,3,8,1,128]{5,1,4,3,0,2:T(4,128)} %slice.548), channel_id=1, source_target_pairs={{16,0},{32,16},{48,32},{64,48},{80,64},{96,80},{112,96},{128,112},... | collective-permute-start | bytes 294920 | tf_op jit(solution)/shard_map/ppermute | solution.py:20
  16.4 0.7 slice.537
  17.1 1.3 collective-permute-start.1
  18.4 1.8 %copy.59 = f32[2,4,3,8,16,1]{4,3,5,2,1,0:T(8,128)} copy(f32[2,4,3,8,16,1]{5,4,3,2,1,0:T(8,128)S(1)} %bitcast.233) | data formatting | bytes 24576
  20.2 1.7 collective-permute-start
  25.1 1.1 fusion.75
  28.3 0.7 fusion.77
  30.0 1.7 fusion.48
  31.7 1.7 fusion.46
  33.4 1.8 %convolution_subtract_fusion.1 = f32[4,49152]{1,0:T(4,128)S(1)} fusion(f32[4,49152]{1,0:T(4,128)S(1)} %fusion.48, f32[4,49152]{1,0:T(4,128)S(1)} %bitcast.237, f32[2,4,4]{2,1,0:T(4,128)S(1)} %copy-done.18), kind=kOutput, calls=%fused_computation.3 | convolution fusion | flops 9633792 | bytes 2361344 | tf_op jit(solution)/shard_map/ab,am->bm/dot_general | solution.py:98
  35.2 1.8 %convolution_add_fusion.1 = f32[4,49152]{1,0:T(4,128)S(1)} fusion(f32[4,49152]{1,0:T(4,128)S(1)} %fusion.46, f32[4,49152]{1,0:T(4,128)S(1)} %bitcast.235, f32[2,4,4]{2,1,0:T(4,128)S(1)} %copy-done.18), kind=kOutput, calls=%fused_computation.2 | convolution fusion | flops 9633792 | bytes 2361344 | tf_op jit(solution)/shard_map/ab,am->bm/dot_general | solution.py:101
  37.6 1.2 pad_maximum_fusion
  38.9 2.5 %select_add_fusion.1 = (f32[8,16,128]{2,1,0:T(8,128)S(1)}, pred[8,16,128]{2,1,0:T(8,128)(4,1)S(1)}, pred[8,16,128]{2,1,0:T(8,128)(4,1)S(1)}, pred[8,16,128]{2,1,0:T(8,128)(4,1)S(1)}, pred[8,16,128]{2,1,0:T(8,128)(4,1)S(1)}) fusion(f32[]{:T(128)} %bitcast.41, f32[]{:T(128)} %bitcast.40, f32[]{:T(128)} %bitcast.39, f32[]{:T(128)} %bitcast.38, ...), kind=kLoop, calls=%fused_computation.116 | loop fusion | flops 180224 | bytes 196624 | tf_op jit(solution)/shard_map/add | solution.py:135
  41.4 2.5 %select_add_fusion = f32[8,16,128]{2,1,0:T(8,128)S(1)} fusion(pred[8,16,128]{2,1,0:T(8,128)(4,1)S(1)} %get-tuple-element.17, pred[8,16,128]{2,1,0:T(8,128)(4,1)S(1)} %get-tuple-element.16, pred[8,16,128]{2,1,0:T(8,128)(4,1)S(1)} %get-tuple-element.15, pred[8,16,128]{2,1,0:T(8,128)(4,1)S(1)} %get-tuple-element.14, f32[]{:T(128)} %bitcast.45, f32[]{:T(128)} %bitcast.44, ...), kind=kLoop, calls=%fused_computation.115 | loop fusion | flops 114688 | bytes 131088 | tf_op jit(solution)/shard_map/add | solution.py:136
  44.0 2.5 %multiply_subtract_fusion.2 = (f32[1,4,1,8,16,128]{5,1,4,3,2,0:T(4,128)}, f32[1,4,1,8,16,128]{5,1,4,3,2,0:T(4,128)}, f32[1,4,1,8,16,128]{5,1,4,3,2,0:T(4,128)}, ...) fusion(f32[1,4,1,8,16,128]{5,4,3,2,1,0:T(8,128)S(1)} %copy-done.9, ...), kind=kLoop, calls=%fused_computation.96 | loop fusion | flops 1179648 | bytes 3276800 | tf_op jit(solution)/shard_map/sub | solution.py:39
  46.5 1.0 copy.70
  47.5 0.9 copy.71
  48.4 14.3 %copy.34 = f32[2,4,3,8,16,1]{5,1,4,3,0,2:T(4,128)} copy(f32[2,4,3,8,16,1]{4,3,5,2,1,0:T(8,128)S(1)} %collective-permute-done) | data formatting | bytes 24576 | tf_op jit(solution)/shard_map/ppermute | solution.py:20
  62.7 1.8 %maximum_bitcast_fusion.1 = (f32[2,4,8,16,129]{4,1,3,2,0:T(4,128)S(1)}, f32[2,4,8,16,129]{4,1,3,2,0:T(4,128)S(1)}) fusion(f32[2,4,3,8,16,1]{5,1,4,3,0,2:T(4,128)} %copy.34, f32[2,4,3,8,16,128]{5,1,4,3,0,2:T(4,128)S(1)} %copy-done.2), kind=kLoop, calls=%fused_computation.31 | loop fusion | flops 264192 | bytes 2641920 | tf_op jit(solution)/shard_map/squeeze | solution.py:61
  65.3 1.2 copy-done.3
  66.5 0.9 constant_dynamic-update-slice_fusion.2
  68.5 0.8 copy-done.4
  69.3 1.0 constant_dynamic-update-slice_fusion
  72.1 2.0 %slice.563 = f32[2,4,3,8,16,1]{5,1,4,3,0,2:T(4,128)} slice(f32[2,4,3,8,16,128]{5,1,4,3,0,2:T(4,128)S(1)} %pad_maximum_fusion.1), slice={[0:2], [0:4], [0:3], [0:8], [0:16], [127:128]} | slice | bytes 24576 | tf_op jit(solution)/shard_map/slice | solution.py:159
  74.1 3.0 %copy.43 = f32[2,4,3,8,16,1]{4,3,5,2,1,0:T(8,128)} copy(f32[2,4,3,8,16,1]{5,1,4,3,0,2:T(4,128)} %slice.563) | data formatting | bytes 24576 | tf_op jit(solution)/shard_map/slice | solution.py:159
  77.1 5.2 %collective-permute-start.3 = (f32[2,4,3,8,16,1]{4,3,5,2,1,0:T(8,128)}, f32[2,4,3,8,16,1]{4,3,5,2,1,0:T(8,128)}, u32[]{:S(2)}, u32[]{:S(2)}) collective-permute-start(f32[2,4,3,8,16,1]{4,3,5,2,1,0:T(8,128)} %copy.43), channel_id=1, source_target_pairs={{0,2},{2,4},{4,6},{6,8},{8,10},{10,12},{12,14},{1,3},{3,5},{5,7},{... | collective-permute-start | bytes 36872 | tf_op jit(solution)/shard_map/ppermute | solution.py:20
  82.9 5.9 %collective-permute-start.4 = (f32[2,4,3,1,16,128]{5,1,4,3,0,2:T(4,128)S(1)}, f32[2,4,3,1,16,128]{5,1,4,3,0,2:T(4,128)}, u32[]{:S(2)}, u32[]{:S(2)}) collective-permute-start(f32[2,4,3,1,16,128]{5,1,4,3,0,2:T(4,128)S(1)} %pad_maximum_fusion.13), channel_id=1, source_target_pairs={{0,1},{2,3},{4,5},{6,7},{8,9},{10,11},{12,13},{14,15},{16,17},{18,... | collective-permute-start | bytes 589832 | tf_op jit(solution)/shard_map/ppermute | solution.py:20
  88.9 1.9 %collective-permute-start.5 = (f32[2,4,3,8,1,128]{5,1,4,3,0,2:T(4,128)}, f32[2,4,3,8,1,128]{5,1,4,3,0,2:T(4,128)S(1)}, u32[]{:S(2)}, u32[]{:S(2)}) collective-permute-start(f32[2,4,3,8,1,128]{5,1,4,3,0,2:T(4,128)} %pad_maximum_fusion.14), channel_id=1, source_target_pairs={{0,16},{16,32},{32,48},{48,64},{64,80},{80,96},{96,112},{112,128},... | collective-permute-start | bytes 294920 | tf_op jit(solution)/shard_map/ppermute | solution.py:20
  90.8 2.9 %copy.44 = f32[2,4,3,8,16,1]{5,1,4,3,0,2:T(4,128)} copy(f32[2,4,3,8,16,1]{4,3,5,2,1,0:T(8,128)} %collective-permute-done.3) | data formatting | bytes 24576 | tf_op jit(solution)/shard_map/ppermute | solution.py:20
  93.7 2.3 %maximum_bitcast_fusion = (f32[2,4,8,16,129]{4,1,3,2,0:T(4,128)S(1)}, f32[2,4,8,16,129]{4,1,3,2,0:T(4,128)S(1)}) fusion(f32[2,4,3,8,16,1]{5,1,4,3,0,2:T(4,128)} %copy.44, f32[2,4,1,8,16,128]{5,1,4,3,0,2:T(4,128)S(1)} %fusion.22, f32[2,4,1,8,16,128]{5,1,4,3,0,2:T(4,128)S(1)} %fusion.21, f32[2,4,1,8,16,128]{5,1,4,3,0,2:T(4,128)S(1)} %fusion.20), kind=kLoop, calls=%fused_computation.28 | loop fusion | flops 792576 | bytes 2641920 | tf_op jit(solution)/shard_map/squeeze | solution.py:61
  97.0 1.6 collective-permute-done.5
  100.4 1.2 maximum_bitcast_fusion.2
  104.1 3.6 %convolution_bitcast_fusion = f32[4,4]{1,0:T(4,128)S(1)} fusion(f32[2,4,3,8,16,128]{5,1,4,3,2,0:T(4,128)S(1)} %pad_maximum_fusion.2, f32[1,4,3,8,16,128]{5,4,3,2,1,0:T(8,128)S(1)} %get-tuple-element.44), kind=kOutput, calls=%fused_computation.16 | convolution fusion | flops 9437184 | bytes 1572928 | tf_op jit(solution)/shard_map/am,bm->ab/dot_general | solution.py:71
  107.7 3.6 %convolution_bitcast_fusion.2 = f32[4,4]{1,0:T(4,128)S(1)} fusion(f32[2,4,3,8,16,128]{5,1,4,3,2,0:T(4,128)S(1)} %pad_maximum_fusion.2, f32[1,4,3,8,16,128]{5,4,3,2,1,0:T(8,128)S(1)} %get-tuple-element.44), kind=kOutput, calls=%fused_computation.18 | convolution fusion | flops 9437184 | bytes 1572928 | tf_op jit(solution)/shard_map/am,bm->ab/dot_general | solution.py:71
  111.3 3.9 %fusion.7 = f32[4,4]{0,1:T(4,128)S(1)} fusion(f32[4,4]{1,0:T(4,128)S(1)} %convolution_bitcast_fusion, f32[2,4,3,8,16,128]{5,1,4,3,2,0:T(4,128)S(1)} %pad_maximum_fusion.2, f32[1,4,3,8,16,128]{5,4,3,2,1,0:T(8,128)S(1)} %get-tuple-element.43), kind=kOutput, calls=%fused_computation.23 | convolution fusion | flops 9437200 | bytes 1574976 | tf_op jit(solution)/shard_map/am,bm->ab/dot_general | solution.py:71
  115.3 3.6 %fusion.5 = f32[4,4]{0,1:T(4,128)S(1)} fusion(f32[4,4]{1,0:T(4,128)S(1)} %convolution_bitcast_fusion.2, f32[2,4,3,8,16,128]{5,1,4,3,2,0:T(4,128)S(1)} %pad_maximum_fusion.2, f32[1,4,3,8,16,128]{5,4,3,2,1,0:T(8,128)S(1)} %get-tuple-element.43), kind=kOutput, calls=%fused_computation.21 | convolution fusion | flops 9437200 | bytes 1574976 | tf_op jit(solution)/shard_map/am,bm->ab/dot_general | solution.py:71
  118.9 6.4 %all-reduce.4 = (f32[4,4]{0,1:T(4,128)S(1)}, f32[4,4]{0,1:T(4,128)S(1)}) all-reduce(f32[4,4]{0,1:T(4,128)S(1)} %fusion.5, f32[4,4]{0,1:T(4,128)S(1)} %fusion.7), channel_id=1, replica_groups=mesh['gx_0'=2,'gx_1'=8,'gx_2'=2,'gy'=8,'gz'=2] {'gx_0'}, use_global_device_ids=true, to_apply=%region_0.1 | all-reduce | flops 32 | bytes 256 | tf_op jit(solution)/shard_map/psum | solution.py:24
  125.3 14.1 %all-reduce.1 = (f32[4,4]{0,1:T(4,128)S(1)}, f32[4,4]{0,1:T(4,128)S(1)}) all-reduce(f32[4,4]{0,1:T(4,128)S(1)} %get-tuple-element.11, f32[4,4]{0,1:T(4,128)S(1)} %get-tuple-element.12), channel_id=1, replica_groups=mesh['gx_0'=2,'gx_1'=8,'gx_2'=2,'gy'=8,'gz'=2] {'gx_1'}, use_global_device_ids=true, to_apply=%region_1.2 | all-reduce | flops 32 | bytes 256 | tf_op jit(solution)/shard_map/psum | solution.py:24
  139.5 2.5 %all-reduce.3 = (f32[4,4]{0,1:T(4,128)S(1)}, f32[4,4]{0,1:T(4,128)S(1)}) all-reduce(f32[4,4]{0,1:T(4,128)S(1)} %get-tuple-element.5, f32[4,4]{0,1:T(4,128)S(1)} %get-tuple-element.6), channel_id=1, replica_groups=mesh['gx_0'=2,'gx_1'=8,'gx_2'=2,'gy'=8,'gz'=2] {'gx_2'}, use_global_device_ids=true, to_apply=%region_2.3 | all-reduce | flops 32 | bytes 256 | tf_op jit(solution)/shard_map/psum | solution.py:24
  141.9 16.4 %all-reduce = (f32[4,4]{0,1:T(4,128)S(1)}, f32[4,4]{0,1:T(4,128)S(1)}) all-reduce(f32[4,4]{0,1:T(4,128)S(1)} %get-tuple-element.9, f32[4,4]{0,1:T(4,128)S(1)} %get-tuple-element.10), channel_id=1, replica_groups=mesh['gx_0'=2,'gx_1'=8,'gx_2'=2,'gy'=8,'gz'=2] {'gy'}, use_global_device_ids=true, to_apply=%region_3.4 | all-reduce | flops 32 | bytes 256 | tf_op jit(solution)/shard_map/psum | solution.py:24
  158.4 4.9 %all-reduce.2 = (f32[4,4]{0,1:T(4,128)S(1)}, f32[4,4]{0,1:T(4,128)S(1)}) all-reduce(f32[4,4]{0,1:T(4,128)S(1)} %get-tuple-element.3, f32[4,4]{0,1:T(4,128)S(1)} %get-tuple-element.4), channel_id=1, replica_groups=mesh['gx_0'=2,'gx_1'=8,'gx_2'=2,'gy'=8,'gz'=2] {'gz'}, use_global_device_ids=true, to_apply=%region_4.5 | all-reduce | flops 32 | bytes 256 | tf_op jit(solution)/shard_map/psum | solution.py:24
  165.2 1.5 fusion.44
  166.7 1.5 fusion.42
  168.2 1.5 fusion
  169.8 1.5 fusion.1
  171.9 1.4 maximum_subtract_fusion
  (108 shorter events, 15.1 us)
Async XLA Ops:
  0.6 17.7 %copy-start = (f32[2,4,3,8,16,128]{5,4,3,2,1,0:T(8,128)S(1)}, f32[2,4,3,8,16,128]{5,4,3,2,1,0:T(8,128)}, u32[]{:S(2)}) copy-start(f32[2,4,3,8,16,128]{5,4,3,2,1,0:T(8,128)} %param.7) | copy-start | bytes 4718596
  5.3 11.1 %copy-start.1 = (f32[2,4,3,8,16,128]{5,1,4,3,0,2:T(4,128)}, f32[2,4,3,8,16,128]{5,1,4,3,0,2:T(4,128)S(1)}, u32[]{:S(2)}) copy-start(f32[2,4,3,8,16,128]{5,1,4,3,0,2:T(4,128)S(1)} %get-tuple-element.42) | copy-start | bytes 4718596
  5.3 16.6 %copy-start.20 = (s32[6]{0:T(128)S(1)}, s32[6]{0:T(128)}, u32[]{:S(2)}) copy-start(s32[6]{0:T(128)} %param.9) | copy-start | bytes 76
  6.0 59.3 %collective-permute-start.2 = (f32[2,4,3,8,1,128]{5,1,4,3,0,2:T(4,128)}, f32[2,4,3,8,1,128]{5,1,4,3,0,2:T(4,128)}, u32[]{:S(2)}, u32[]{:S(2)}) collective-permute-start(f32[2,4,3,8,1,128]{5,1,4,3,0,2:T(4,128)} %slice.548), channel_id=1, source_target_pairs={{16,0},{32,16},{48,32},{64,48},{80,64},{96,80},{112,96},{128,112},... | collective-permute-start | bytes 294920 | tf_op jit(solution)/shard_map/ppermute | solution.py:20
  17.1 51.4 %collective-permute-start.1 = (f32[2,4,3,1,16,128]{5,1,4,3,0,2:T(4,128)}, f32[2,4,3,1,16,128]{5,1,4,3,0,2:T(4,128)}, u32[]{:S(2)}, u32[]{:S(2)}) collective-permute-start(f32[2,4,3,1,16,128]{5,1,4,3,0,2:T(4,128)} %slice.537), channel_id=1, source_target_pairs={{1,0},{3,2},{5,4},{7,6},{9,8},{11,10},{13,12},{15,14},{17,16},{19,... | collective-permute-start | bytes 589832 | tf_op jit(solution)/shard_map/ppermute | solution.py:20
  20.2 28.2 %collective-permute-start = (f32[2,4,3,8,16,1]{4,3,5,2,1,0:T(8,128)}, f32[2,4,3,8,16,1]{4,3,5,2,1,0:T(8,128)S(1)}, u32[]{:S(2)}, u32[]{:S(2)}) collective-permute-start(f32[2,4,3,8,16,1]{4,3,5,2,1,0:T(8,128)} %copy.59), channel_id=1, source_target_pairs={{2,0},{4,2},{6,4},{8,6},{10,8},{12,10},{14,12},{3,1},{5,3},{7,5},{... | collective-permute-start | bytes 36872 | tf_op jit(solution)/shard_map/ppermute | solution.py:20
  26.2 1.4 copy-start.21
  26.2 2.0 %copy-start.22 = (f32[4]{0:T(128)S(1)}, f32[4]{0:T(128)}, u32[]{:S(2)}) copy-start(f32[4]{0:T(128)} %param.11) | copy-start | bytes 52
  28.9 1.0 copy-start.18
  35.2 1.8 %copy-start.23 = (f32[2,4]{1,0:T(2,128)S(1)}, f32[2,4]{1,0:T(2,128)}, u32[]{:S(2)}) copy-start(f32[2,4]{1,0:T(2,128)} %param.13) | copy-start | bytes 100
  37.5 1.3 copy-start.19
  37.5 6.4 %copy-start.7 = (f32[1,4,1,8,16,128]{5,4,3,2,1,0:T(8,128)S(1)}, f32[1,4,1,8,16,128]{5,4,3,2,1,0:T(8,128)}, u32[]{:S(2)}) copy-start(f32[1,4,1,8,16,128]{5,4,3,2,1,0:T(8,128)} %get-tuple-element.35) | copy-start | bytes 786436
  37.6 6.4 %copy-start.8 = (f32[1,4,1,8,16,128]{5,4,3,2,1,0:T(8,128)S(1)}, f32[1,4,1,8,16,128]{5,4,3,2,1,0:T(8,128)}, u32[]{:S(2)}) copy-start(f32[1,4,1,8,16,128]{5,4,3,2,1,0:T(8,128)} %get-tuple-element.36) | copy-start | bytes 786436
  37.6 6.4 %copy-start.9 = (f32[1,4,1,8,16,128]{5,4,3,2,1,0:T(8,128)S(1)}, f32[1,4,1,8,16,128]{5,4,3,2,1,0:T(8,128)}, u32[]{:S(2)}) copy-start(f32[1,4,1,8,16,128]{5,4,3,2,1,0:T(8,128)} %get-tuple-element.37) | copy-start | bytes 786436
  37.6 6.4 %copy-start.10 = (f32[1,4,1,8,16,128]{5,4,3,2,1,0:T(8,128)S(1)}, f32[1,4,1,8,16,128]{5,4,3,2,1,0:T(8,128)}, u32[]{:S(2)}) copy-start(f32[1,4,1,8,16,128]{5,4,3,2,1,0:T(8,128)} %get-tuple-element.38) | copy-start | bytes 786436
  37.6 6.4 %copy-start.11 = (f32[1,4,1,8,16,128]{5,4,3,2,1,0:T(8,128)S(1)}, f32[1,4,1,8,16,128]{5,4,3,2,1,0:T(8,128)}, u32[]{:S(2)}) copy-start(f32[1,4,1,8,16,128]{5,4,3,2,1,0:T(8,128)} %get-tuple-element.39) | copy-start | bytes 786436
  47.5 15.2 %copy-start.2 = (f32[2,4,3,8,16,128]{5,1,4,3,0,2:T(4,128)S(1)}, f32[2,4,3,8,16,128]{5,1,4,3,0,2:T(4,128)}, u32[]{:S(2)}) copy-start(f32[2,4,3,8,16,128]{5,1,4,3,0,2:T(4,128)} %copy-done.1) | copy-start | bytes 4718596
  65.1 1.4 copy-start.3
  67.8 1.5 copy-start.4
  77.1 13.7 %collective-permute-start.3 = (f32[2,4,3,8,16,1]{4,3,5,2,1,0:T(8,128)}, f32[2,4,3,8,16,1]{4,3,5,2,1,0:T(8,128)}, u32[]{:S(2)}, u32[]{:S(2)}) collective-permute-start(f32[2,4,3,8,16,1]{4,3,5,2,1,0:T(8,128)} %copy.43), channel_id=1, source_target_pairs={{0,2},{2,4},{4,6},{6,8},{8,10},{10,12},{12,14},{1,3},{3,5},{5,7},{... | collective-permute-start | bytes 36872 | tf_op jit(solution)/shard_map/ppermute | solution.py:20
  82.9 17.5 %collective-permute-start.4 = (f32[2,4,3,1,16,128]{5,1,4,3,0,2:T(4,128)S(1)}, f32[2,4,3,1,16,128]{5,1,4,3,0,2:T(4,128)}, u32[]{:S(2)}, u32[]{:S(2)}) collective-permute-start(f32[2,4,3,1,16,128]{5,1,4,3,0,2:T(4,128)S(1)} %pad_maximum_fusion.13), channel_id=1, source_target_pairs={{0,1},{2,3},{4,5},{6,7},{8,9},{10,11},{12,13},{14,15},{16,17},{18,... | collective-permute-start | bytes 589832 | tf_op jit(solution)/shard_map/ppermute | solution.py:20
  88.9 9.7 %collective-permute-start.5 = (f32[2,4,3,8,1,128]{5,1,4,3,0,2:T(4,128)}, f32[2,4,3,8,1,128]{5,1,4,3,0,2:T(4,128)S(1)}, u32[]{:S(2)}, u32[]{:S(2)}) collective-permute-start(f32[2,4,3,8,1,128]{5,1,4,3,0,2:T(4,128)} %pad_maximum_fusion.14), channel_id=1, source_target_pairs={{0,16},{16,32},{32,48},{48,64},{64,80},{80,96},{96,112},{112,128},... | collective-permute-start | bytes 294920 | tf_op jit(solution)/shard_map/ppermute | solution.py:20
  99.0 1.0 copy-start.16
  99.0 1.0 copy-start.17
  101.7 1.0 copy-start.14
  101.7 1.0 copy-start.15
  102.2 1.0 copy-start.12
  102.2 1.1 copy-start.13
  169.7 2.2 %copy-start.5 = (f32[1,4,384,128]{3,2,1,0:T(8,128)S(1)}, f32[1,4,384,128]{3,2,1,0:T(8,128)}, u32[]{:S(2)}) copy-start(f32[1,4,384,128]{3,2,1,0:T(8,128)} %copy.70) | copy-start | bytes 2359300
  169.8 2.2 %copy-start.6 = (f32[1,4,384,128]{3,2,1,0:T(8,128)S(1)}, f32[1,4,384,128]{3,2,1,0:T(8,128)}, u32[]{:S(2)}) copy-start(f32[1,4,384,128]{3,2,1,0:T(8,128)} %copy.71) | copy-start | bytes 2359300
where the time goes:
time: 177 us; the launch traced here: 174 us
  blocking collectives  44.4 us (25%)
  local copies, waits for them, and re-layouts  42.1 us (24%)
  matrix products  29.4 us (17%)
  starting transfers between devices  26.2 us (15%)
  other arithmetic  24.5 us (14%)
  between operations  5.32 us (3%)
    psum x5, blocking collectives, one_axis_at_a_time(): return functools.reduce(lax.psum, axes, shard)  44.4 us
    ppermute x6, starting transfers between devices, passed_along(): lax.ppermute(value, axis, [(source, source + steps) for source in range(l...  26.2 us
    ppermute x2, local copies, waits for them, and re-layouts, passed_along(): lax.ppermute(value, axis, [(source, source + steps) for source in range(l...  17.2 us
    dot_general x4, matrix products, product(): return jnp.einsum('am,bm->ab', left, right, precision=lax.Precision.HIGHEST)  14.9 us
    unnamed x58, local copies, waits for them, and re-layouts  13 us
    squeeze x4, other arithmetic, derivative(): values = extended[direction][:, :, number]  5.55 us
    slice x2, local copies, waits for them, and re-layouts, body(): lax.slice_in_dim(magnetic, counts[2] - 1, counts[2], axis=5)  5.03 us
  transfers between devices with their start and end apart: 6, of which 1 were waited for; matrix products, arithmetic and copies ran while one was open for 30% of the time, Pallas kernels for 0%

commit v1 on v0

v1 whole, which is shorter than its diff:
```python
import functools

import jax
import jax.numpy as jnp
from jax import lax
from jax.experimental import pallas as pl
from jax.experimental.pallas import tpu as pltpu
from jax.sharding import Mesh
from jax.sharding import PartitionSpec as P

GX = ("xh", "zz", "core")
OMEGA_SQ = 0.36
SIGMA_TOP = 3.0
NV = 4
MESH = pl.DeviceIdType.MESH
PAIRS = [(a, b) for a in range(NV) for b in range(a, NV)]


def inverse_stretch(places, length, low_width, high_width):
    inside_depth = jnp.clip((low_width - places) / low_width, 0.0, 1.0) + jnp.clip(
        (places + 1.0 - length + high_width) / high_width, 0.0, 1.0
    )
    absorb = SIGMA_TOP * inside_depth * inside_depth
    scaled = 1.0 / (1.0 + absorb * absorb)
    return scaled, -absorb * scaled


def cmul(f, v):
    return (f[0] * v[0] - f[1] * v[1], f[0] * v[1] + f[1] * v[0])


def csub(p, q):
    return (p[0] - q[0], p[1] - q[1])


def curl(dx, dy, dz):
    return (
        csub(dy[2], dz[1]),
        csub(dz[0], dx[2]),
        csub(dx[1], dy[0]),
    )


def fold(x):
    return x[0:8] + x[8:16]


def kernel(
    sizes,
    pml_hbm, eps_r_hbm, eps_l_hbm, coef_hbm, ritz_hbm, mat_hbm, fields,
    basis, resid, gram,
    pml, eps_r, eps_l, coef, ritz, mat, v, h, gs, acc, sym, eps, sxy, sz,
    send_x, send_y, up_xh, up_yh, up_zh,
    hsend_x, hsend_y, dn_xh, dn_yh, dn_zh,
    buf1, buf2, buf3,
    small_sem, load_sem, halo_send, halo_recv, ss1, rs1, ss2, rs2, ss3, rs3,
):
    nz, nx, ny, n_gx, n_gy, n_gz, n_zz = sizes
    n_x = n_gx // (2 * n_zz)
    xh, zz, core = (lax.axis_index(name) for name in GX)
    gy, gz = lax.axis_index("gy"), lax.axis_index("gz")
    gx = (xh * n_zz + zz) * 2 + core
    n1 = n_x * n_gz * 2
    g1 = (xh * n_gz + gz) * 2 + core

    def gx_id(index):
        return {"xh": index // (2 * n_zz), "zz": (index // 2) % n_zz, "core": index % 2}

    def g1_id(index):
        return {"xh": index // (2 * n_gz), "gz": (index // 2) % n_gz, "core": index % 2}

    gx_up, gx_dn = (gx + 1) % n_gx, (gx + n_gx - 1) % n_gx
    gy_up, gy_dn = (gy + 1) % n_gy, (gy + n_gy - 1) % n_gy

    barrier = pltpu.get_barrier_semaphore()

    def greet(device_id):
        pl.semaphore_signal(barrier, inc=1, device_id=device_id, device_id_type=MESH)

    for d in range(1, n1):
        greet(g1_id((g1 + d) % n1))
    for d in range(1, n_gy):
        greet({"gy": (gy + d) % n_gy})
    for d in range(1, n_zz):
        greet({"zz": (zz + d) % n_zz})
    greet(gx_id(gx_up))
    greet(gx_id(gx_dn))
    greetings = n1 - 1 + n_gy - 1 + n_zz - 1 + 2

    smalls = [
        pltpu.make_async_copy(src, dst, small_sem.at[k])
        for k, (src, dst) in enumerate(
            (
                (coef_hbm, coef), (pml_hbm, pml), (eps_r_hbm, eps_r),
                (eps_l_hbm, eps_l), (ritz_hbm, ritz), (mat_hbm, mat),
            )
        )
    ]
    for copy in smalls:
        copy.start()

    def load(z):
        return pltpu.make_async_copy(
            fields.at[:, :, :, z], v.at[:, :, :, z], load_sem.at[z]
        )

    for z in range(nz):
        load(z).start()
    for copy in smalls:
        copy.wait()

    row16 = lax.broadcasted_iota(jnp.int32, (16, 128), 0)
    lane16 = lax.broadcasted_iota(jnp.int32, (16, 128), 1)
    lane8 = lax.broadcasted_iota(jnp.int32, (8, 128), 1)
    row8 = lax.broadcasted_iota(jnp.int32, (8, 128), 0)

    def width(slot):
        return jnp.full((8, 128), pml[slot], jnp.int32).astype(jnp.float32)

    def put(kind, places, length, low, high):
        value = inverse_stretch(places, float(length), low, high)
        sxy[kind, 0] = value[0]
        sxy[kind, 1] = value[1]

    px = (row16 + gx * nx).astype(jnp.float32)
    py = (lane16 + gy * ny).astype(jnp.float32)
    twice = lambda t: jnp.concatenate([t, t], axis=0)
    lx, hx_w, ly, hy_w = (twice(width(slot)) for slot in range(4))
    total_x, total_y, total_z = nx * n_gx, ny * n_gy, nz * n_gz
    put(0, px + 0.5, total_x, lx, hx_w)
    put(1, px, total_x, lx, hx_w)
    put(2, px + 1.0, total_x, lx, hx_w)
    put(3, py + 0.5, total_y, ly, hy_w)
    put(4, py, total_y, ly, hy_w)
    put(5, py + 1.0, total_y, ly, hy_w)
    lz, hz_w = width(4), width(5)

    def z_stretch(z, carry):
        places = jnp.full((8, 128), z + gz * nz, jnp.int32).astype(jnp.float32)
        for kind, shift in ((0, 0.5), (1, 0.0)):
            value = inverse_stretch(places + shift, float(total_z), lz, hz_w)
            sz[kind, 0, z] = value[0]
            sz[kind, 1, z] = value[1]
        return carry

    lax.fori_loop(0, nz + 1, z_stretch, 0)

    for c in range(2):
        for a in range(NV):
            for b in range(NV):
                acc[c, a, b] = jnp.zeros((8, 128), jnp.float32)
        for k in range(len(PAIRS)):
            sym[c, k] = jnp.zeros((8, 128), jnp.float32)

    def rotate(z, packed):
        load(z).wait()
        packed = list(packed)
        for comp in range(3):
            vr = [v[0, a, comp, z] for a in range(NV)]
            vi = [v[1, a, comp, z] for a in range(NV)]
            for b in range(NV):
                re = im = None
                for a in range(NV):
                    cr, ci = coef[0, a, b], coef[1, a, b]
                    pr = cr * vr[a] - ci * vi[a]
                    pi = cr * vi[a] + ci * vr[a]
                    re = pr if re is None else re + pr
                    im = pi if im is None else im + pi
                for c, value in ((0, re), (1, im)):
                    basis[c, b, comp, z] = value
                    if comp != 0:
                        send_x[c, b, comp - 1, pl.ds(z, 1), :] = value[0:1]
                    if comp != 1:
                        slot = comp // 2
                        for t in range(2):
                            place = (c * NV + b) * 16 + 2 * z + t
                            first = jnp.broadcast_to(value[8 * t : 8 * t + 8, 0:1], (8, 128))
                            packed[slot] = jnp.where(lane8 == place, first, packed[slot])
        return tuple(packed)

    zero8 = jnp.zeros((8, 128), jnp.float32)
    packed = lax.fori_loop(0, nz, rotate, (zero8, zero8))
    send_y[0] = packed[0]
    send_y[1] = packed[1]

    pl.semaphore_wait(barrier, greetings)

    def remote(src, dst, slot, device_id):
        return pltpu.make_async_remote_copy(
            src_ref=src, dst_ref=dst, send_sem=halo_send.at[slot], recv_sem=halo_recv.at[slot],
            device_id=device_id, device_id_type=MESH,
        )

    up_z = remote(basis.at[:, :, 0:2, 0], up_zh, 0, {"gz": 0})
    up_x = remote(send_x, up_xh, 1, gx_id(gx_dn))
    up_y = remote(send_y, up_yh, 2, {"gy": gy_dn})

    @pl.when(gz == 1)
    def _():
        up_z.start()

    up_x.start()
    up_y.start()

    def local_gram(z, carry):
        m = mat[z]

        def pick(table):
            low = jnp.where(m == 0, table[0], table[1])
            return OMEGA_SQ * jnp.where(m < 2, low, jnp.where(m == 2, table[2], table[3]))

        er, ei = pick(eps_r), pick(eps_l)
        eps[0, z] = er
        eps[1, z] = ei
        for a in range(NV):
            q = [cmul((er, ei), (basis[0, a, comp, z], basis[1, a, comp, z])) for comp in range(3)]
            for b in range(a, NV):
                k = PAIRS.index((a, b))
                re = im = None
                for comp in range(3):
                    pr, pi = cmul(q[comp], (basis[0, b, comp, z], basis[1, b, comp, z]))
                    re = pr if re is None else re + pr
                    im = pi if im is None else im + pi
                sym[0, k] += fold(re)
                sym[1, k] += fold(im)
        return carry

    lax.fori_loop(0, nz, local_gram, 0)

    up_x.wait_recv()
    up_y.wait_recv()

    @pl.when(gx == n_gx - 1)
    def _():
        up_xh[...] = jnp.zeros(up_xh.shape, jnp.float32)

    @pl.when(gy == n_gy - 1)
    def _():
        up_yh[...] = jnp.zeros(up_yh.shape, jnp.float32)

    def pair(ref, *index):
        return ref[(0,) + index], ref[(1,) + index]

    def stretch(kind):
        return sxy[kind, 0], sxy[kind, 1]

    def stretch_z(kind, z):
        return twice(sz[kind, 0, z]), twice(sz[kind, 1, z])

    def unpacked(ref, slot, c, b, z, lane):
        parts = []
        for t in range(2):
            place = (c * NV + b) * 16 + 2 * z + t
            parts.append(pltpu.roll(ref[slot], (lane - place) % 128, 1))
        return jnp.concatenate(parts, axis=0)

    def forward(z, next_z):
        for b in range(NV):
            f = [pair(basis, b, comp, z) for comp in range(3)]

            def both(comp, ahead, sh, se, se_next):
                d = csub(ahead, f[comp])
                return cmul(sh, d), csub(cmul(se_next, ahead), cmul(se, f[comp]))

            dx, dy, dz = {}, {}, {}
            for comp in (1, 2):
                ahead = tuple(
                    jnp.where(
                        row16 == 15,
                        up_xh[c, b, comp - 1, pl.ds(z, 1), :],
                        pltpu.roll(f[comp][c], 15, 0),
                    )
                    for c in range(2)
                )
                dx[comp] = both(comp, ahead, stretch(0), stretch(1), stretch(2))
            for comp in (0, 2):
                ahead = tuple(
                    jnp.where(
                        lane16 == 127,
                        unpacked(up_yh, comp // 2, c, b, z, 127),
                        pltpu.roll(f[comp][c], 127, 1),
                    )
                    for c in range(2)
                )
                dy[comp] = both(comp, ahead, stretch(3), stretch(4), stretch(5))
            for comp in (0, 1):
                ahead = next_z(b, comp)
                dz[comp] = both(
                    comp, ahead, stretch_z(0, z), stretch_z(1, z), stretch_z(1, z + 1)
                )
            for part, where in ((0, "h"), (1, "g")):
                turned = curl(*({k: t[part] for k, t in d.items()} for d in (dx, dy, dz)))
                for comp in range(3):
                    for c in range(2):
                        if where == "h":
                            h[c, b, comp, z] = turned[comp][c]
                        else:
                            gs[c, b, comp] = turned[comp][c]
        for b in range(NV):
            hb = [pair(h, b, comp, z) for comp in range(3)]
            for a in range(NV):
                re = im = None
                for comp in range(3):
                    pr, pi = cmul(pair(gs, a, comp), hb[comp])
                    re = pr if re is None else re + pr
                    im = pi if im is None else im + pi
                acc[0, a, b] += fold(re)
                acc[1, a, b] += fold(im)

    def forward_step(z, carry):
        forward(z, lambda b, comp: pair(basis, b, comp, z + 1))
        return carry

    lax.fori_loop(0, nz - 1, forward_step, 0)

    @pl.when(gz == 0)
    def _():
        up_z.wait_recv()

    @pl.when(gz == 1)
    def _():
        up_zh[...] = jnp.zeros(up_zh.shape, jnp.float32)

    forward(nz - 1, lambda b, comp: pair(up_zh, b, comp))

    tile = zero8
    for b in range(NV):
        rows = zero8
        for c in range(2):
            for a in range(NV):
                s = acc[c, a, b] - sym[c, PAIRS.index((min(a, b), max(a, b)))]
                s = jnp.sum(s, axis=0, keepdims=True)
                rows = jnp.where(row8 == c * NV + a, s, rows)
        total = jnp.sum(rows, axis=1, keepdims=True)
        tile = jnp.where(lane8 == b, total, tile)

    def exchange(buf, count, me, ids, ss, rs):
        copies = []
        for d in range(1, count):
            peer = (me + d) % count
            copies.append(
                pltpu.make_async_remote_copy(
                    src_ref=buf.at[me], dst_ref=buf.at[me], send_sem=ss.at[d], recv_sem=rs.at[me],
                    device_id=ids(peer), device_id_type=MESH,
                )
            )
        for copy in copies:
            copy.start()

        def arrived():
            for d in range(1, count):
                peer = (me + d) % count
                pltpu.make_async_remote_copy(
                    src_ref=buf.at[peer], dst_ref=buf.at[peer], send_sem=ss.at[d],
                    recv_sem=rs.at[peer], device_id=ids(peer), device_id_type=MESH,
                ).wait_recv()
            total = buf[0]
            for k in range(1, count):
                total = total + buf[k]
            return total

        def sent():
            for copy in copies:
                copy.wait_send()

        return arrived, sent

    buf1[g1] = tile
    arrived1, sent1 = exchange(buf1, n1, g1, g1_id, ss1, rs1)

    def pack(z, packed):
        packed = list(packed)
        for b in range(NV):
            for c in range(2):
                for comp in range(3):
                    value = h[c, b, comp, z]
                    if comp != 0:
                        hsend_x[c, b, comp - 1, pl.ds(z, 1), :] = value[15:16]
                    if comp != 1:
                        slot = comp // 2
                        for t in range(2):
                            place = (c * NV + b) * 16 + 2 * z + t
                            last = jnp.broadcast_to(value[8 * t : 8 * t + 8, 127:128], (8, 128))
                            packed[slot] = jnp.where(lane8 == place, last, packed[slot])
        return tuple(packed)

    packed = lax.fori_loop(0, nz, pack, (zero8, zero8))
    hsend_y[0] = packed[0]
    hsend_y[1] = packed[1]
    dn_z = remote(h.at[:, :, 0:2, nz - 1], dn_zh, 3, {"gz": 1})
    dn_x = remote(hsend_x, dn_xh, 4, gx_id(gx_up))
    dn_y = remote(hsend_y, dn_yh, 5, {"gy": gy_up})

    @pl.when(gz == 0)
    def _():
        dn_z.start()

    dn_x.start()
    dn_y.start()

    buf2[gy] = arrived1()
    arrived2, sent2 = exchange(buf2, n_gy, gy, lambda k: {"gy": k}, ss2, rs2)

    dn_x.wait_recv()
    dn_y.wait_recv()

    @pl.when(gz == 1)
    def _():
        dn_z.wait_recv()

    @pl.when(gz == 0)
    def _():
        dn_zh[...] = jnp.zeros(dn_zh.shape, jnp.float32)

    @pl.when(gx == 0)
    def _():
        dn_xh[...] = jnp.zeros(dn_xh.shape, jnp.float32)

    @pl.when(gy == 0)
    def _():
        dn_yh[...] = jnp.zeros(dn_yh.shape, jnp.float32)

    def backward(z, behind_z):
        er, ei = eps[0, z], eps[1, z]
        for b in range(NV):
            f = [pair(h, b, comp, z) for comp in range(3)]
            dx, dy, dz = {}, {}, {}
            for comp in (1, 2):
                behind = tuple(
                    jnp.where(
                        row16 == 0,
                        dn_xh[c, b, comp - 1, pl.ds(z, 1), :],
                        pltpu.roll(f[comp][c], 1, 0),
                    )
                    for c in range(2)
                )
                dx[comp] = cmul(stretch(1), csub(f[comp], behind))
            for comp in (0, 2):
                behind = tuple(
                    jnp.where(
                        lane16 == 0,
                        unpacked(dn_yh, comp // 2, c, b, z, 128),
                        pltpu.roll(f[comp][c], 1, 1),
                    )
                    for c in range(2)
                )
                dy[comp] = cmul(stretch(4), csub(f[comp], behind))
            for comp in (0, 1):
                dz[comp] = cmul(stretch_z(1, z), csub(f[comp], behind_z(b, comp)))
            turned = curl(dx, dy, dz)
            shifted = (er + ritz[0, b], ei + ritz[1, b])
            for comp in range(3):
                out = csub(turned[comp], cmul(shifted, pair(basis, b, comp, z)))
                resid[0, b, comp, z] = out[0]
                resid[1, b, comp, z] = out[1]

    backward(0, lambda b, comp: pair(dn_zh, b, comp))

    def backward_step(z, carry):
        backward(z, lambda b, comp: pair(h, b, comp, z - 1))
        return carry

    lax.fori_loop(1, nz, backward_step, 0)

    buf3[zz] = arrived2()
    arrived3, sent3 = exchange(buf3, n_zz, zz, lambda k: {"zz": k}, ss3, rs3)

    @pl.when(gz == 1)
    def _():
        up_z.wait_send()

    @pl.when(gz == 0)
    def _():
        dn_z.wait_send()

    for copy in (up_x, up_y, dn_x, dn_y):
        copy.wait_send()
    sent1()
    sent2()
    final = arrived3() * (1.0 / (3.0 * total_x * total_y * total_z))
    gram[0] = final[0:NV, 0:NV]
    gram[1] = final[NV : 2 * NV, 0:NV]
    sent3()


def body(sizes, fields, material, pml_width, eps_real, eps_loss, coeffs, ritz):
    nz, nx, ny, n_gx, n_gy, n_gz, n_zz = sizes
    n1 = n_gx // n_zz * n_gz
    whole = fields.shape
    f32 = jnp.float32
    vmem = pl.BlockSpec(memory_space=pltpu.VMEM)
    face_x = pltpu.VMEM((2, NV, 2, nz, ny), f32)
    face_y = pltpu.VMEM((2, 8, 128), f32)
    face_z = pltpu.VMEM((2, NV, 2, nx, ny), f32)
    dma = pltpu.SemaphoreType.DMA
    return pl.pallas_call(
        functools.partial(kernel, sizes),
        out_shape=(
            jax.ShapeDtypeStruct(whole, f32),
            jax.ShapeDtypeStruct(whole, f32),
            jax.ShapeDtypeStruct((2, NV, NV), f32),
        ),
        in_specs=[pl.BlockSpec(memory_space=pltpu.HBM)] * 7,
        out_specs=(vmem, vmem, vmem),
        scratch_shapes=[
            pltpu.SMEM((6,), jnp.int32),
            pltpu.SMEM((4,), f32),
            pltpu.SMEM((4,), f32),
            pltpu.SMEM((2, NV, NV), f32),
            pltpu.SMEM((2, NV), f32),
            pltpu.VMEM((nz, nx, ny), jnp.int32),
            pltpu.VMEM(whole, f32),
            pltpu.VMEM(whole, f32),
            pltpu.VMEM((2, NV, 3, nx, ny), f32),
            pltpu.VMEM((2, NV, NV, 8, 128), f32),
            pltpu.VMEM((2, len(PAIRS), 8, 128), f32),
            pltpu.VMEM((2, nz, nx, ny), f32),
            pltpu.VMEM((6, 2, nx, ny), f32),
            pltpu.VMEM((2, 2, nz + 1, 8, 128), f32),
            face_x, face_y, face_x, face_y, face_z,
            face_x, face_y, face_x, face_y, face_z,
            pltpu.VMEM((n1, 8, 128), f32),
            pltpu.VMEM((n_gy, 8, 128), f32),
            pltpu.VMEM((n_zz, 8, 128), f32),
            dma((6,)),
            dma((nz,)),
            dma((6,)),
            dma((6,)),
            dma((n1,)), dma((n1,)),
            dma((n_gy,)), dma((n_gy,)),
            dma((n_zz,)), dma((n_zz,)),
        ],
        compiler_params=pltpu.CompilerParams(
            collective_id=0, has_side_effects=True, vmem_limit_bytes=24 * 1024 * 1024
        ),
    )(*(pltpu.with_memory_space_constraint(x, pltpu.HBM) for x in (pml_width, eps_real, eps_loss, coeffs, ritz, material, fields)))


def solution(mesh):
    n_gx, n_gy, n_gz = mesh.shape["gx"], mesh.shape["gy"], mesh.shape["gz"]
    n_zz = n_gx // 4
    split = Mesh(
        mesh.devices.reshape(2, n_zz, 2, n_gy, n_gz),
        ("xh", "zz", "core", "gy", "gz"),
    )
    sizes = (16 // n_gz, 512 // n_gx, 1024 // n_gy, n_gx, n_gy, n_gz, n_zz)
    placed = (P(None, None, None, "gz", GX, "gy"), P("gz", GX, "gy"), P(), P(), P(), P(), P())
    return jax.shard_map(
        functools.partial(body, sizes),
        mesh=split,
        in_specs=placed,
        out_specs=(P(None, None, None, "gz", GX, "gy"), P(None, None, None, "gz", GX, "gy"), P()),
        check_vma=False,
    )
```

time: 177 us -> 36.9 us (0.21)
  the two profiles are of different devices: /device:TPU:4 before, /device:TPU:1 now
where the time goes in v1:
time: 36.9 us; the launch traced here: 36.8 us
  Pallas kernels  33.3 us (90%)
  local copies, waits for them, and re-layouts  2.88 us (8%)
  between operations  0.64 us (2%)
    pallas_call x1, Pallas kernels, body(): pl.pallas_call(functools.partial(kernel, sizes), out_shape=(jax.ShapeDtyp...  33.3 us
    unnamed x3, local copies, waits for them, and re-layouts  2.88 us

profile of v1, /device:TPU:1, one launch (start us, length us, event | category | flops | bytes accessed | tf_op | source)
XLA Modules:
  0.0 36.8 jit_solution(7540830004304825168)
XLA Ops:
  0.6 33.3 %shard_map.94 = (f32[2,4,3,8,16,128]{5,4,3,2,1,0:T(8,128)S(1)}, f32[2,4,3,8,16,128]{5,4,3,2,1,0:T(8,128)S(1)}, f32[2,4,4]{2,1,0:T(4,128)S(1)}) custom-call(s32[6]{0:T(128)} %pml_hbm.1, f32[4]{0:T(128)} %eps_r_hbm.1, f32[4]{0:T(128)} %eps_l_hbm.1, f32[2,4,4]{2,1,0:T(4,128)} %coef_hbm.1, f32[2,4]{1,0:T(2,128)} %ritz_hbm.1, s32[8,16,128]{2,1,0:T(8,128)} %mat_hbm.1, ...), custom_call_target="tpu_custom_call" | custom-call | tf_op jit(solution)/shard_map/pallas_call | solution.py:496
  33.9 1.1 %copy.13 = f32[2,4,3,8,16,128]{5,4,3,2,1,0:T(8,128)} copy(f32[2,4,3,8,16,128]{5,4,3,2,1,0:T(8,128)S(1)} %get-tuple-element.6) | data formatting | bytes 3145728
  35.1 1.1 %copy.14 = f32[2,4,3,8,16,128]{5,4,3,2,1,0:T(8,128)} copy(f32[2,4,3,8,16,128]{5,4,3,2,1,0:T(8,128)S(1)} %get-tuple-element.7) | data formatting | bytes 3145728
  36.2 0.6 %copy.15 = f32[2,4,4]{2,1,0:T(4,128)} copy(f32[2,4,4]{2,1,0:T(4,128)S(1)} %get-tuple-element.8) | data formatting | bytes 256

commit v2 on v1

--- a/solution.py
+++ b/solution.py
@@ -50,10 +50,10 @@
     pml_hbm, eps_r_hbm, eps_l_hbm, coef_hbm, ritz_hbm, mat_hbm, fields,
     basis, resid, gram,
     pml, eps_r, eps_l, coef, ritz, mat, v, h, gs, acc, sym, eps, sxy, sz,
-    send_x, send_y, up_xh, up_yh, up_zh,
+    send_x, send_y, up_xh, up_yh, up_raw, up_zh,
     hsend_x, hsend_y, dn_xh, dn_yh, dn_zh,
     buf1, buf2, buf3,
-    small_sem, load_sem, halo_send, halo_recv, ss1, rs1, ss2, rs2, ss3, rs3,
+    small_sem, load_sem, halo_send, halo_recv, ss1, rs1, ss2, rs2, ss3, rs3, near, far,
 ):
     nz, nx, ny, n_gx, n_gy, n_gz, n_zz = sizes
     n_x = n_gx // (2 * n_zz)
@@ -71,21 +71,6 @@
 
     gx_up, gx_dn = (gx + 1) % n_gx, (gx + n_gx - 1) % n_gx
     gy_up, gy_dn = (gy + 1) % n_gy, (gy + n_gy - 1) % n_gy
-
-    barrier = pltpu.get_barrier_semaphore()
-
-    def greet(device_id):
-        pl.semaphore_signal(barrier, inc=1, device_id=device_id, device_id_type=MESH)
-
-    for d in range(1, n1):
-        greet(g1_id((g1 + d) % n1))
-    for d in range(1, n_gy):
-        greet({"gy": (gy + d) % n_gy})
-    for d in range(1, n_zz):
-        greet({"zz": (zz + d) % n_zz})
-    greet(gx_id(gx_up))
-    greet(gx_id(gx_dn))
-    greetings = n1 - 1 + n_gy - 1 + n_zz - 1 + 2
 
     smalls = [
         pltpu.make_async_copy(src, dst, small_sem.at[k])
@@ -99,15 +84,50 @@
     for copy in smalls:
         copy.start()
 
-    def load(z):
-        return pltpu.make_async_copy(
-            fields.at[:, :, :, z], v.at[:, :, :, z], load_sem.at[z]
+    for c in range(2):
+        for a in range(NV):
+            pltpu.make_async_copy(fields.at[c, a], v.at[c, a], load_sem).start()
+
+    barrier = pltpu.get_barrier_semaphore()
+
+    def signal(sem, device_id):
+        pl.semaphore_signal(sem, inc=1, device_id=device_id, device_id_type=MESH)
+
+    def beside(step):
+        return (
+            {"gy": (gy + step) % n_gy},
+            {"gy": (gy + n_gy - step) % n_gy},
+            {"zz": (zz + step) % n_zz},
+            {"zz": (zz + n_zz - step) % n_zz},
         )
 
-    for z in range(nz):
-        load(z).start()
+    greeted = [gx_id(gx_up), gx_id(gx_dn)] + list(beside(1))
+    greeted += [g1_id((g1 + d) % n1) for d in range(1, n1)]
+    for device_id in greeted:
+        signal(barrier, device_id)
+
+    def remote(src, dst, slot, device_id):
+        return pltpu.make_async_remote_copy(
+            src_ref=src, dst_ref=dst, send_sem=halo_send.at[slot], recv_sem=halo_recv.at[slot],
+            device_id=device_id, device_id_type=MESH,
+        )
+
+    up_z = remote(fields.at[:, :, 0:2, 0], up_raw, 0, {"gz": 0})
+    up_x = remote(send_x, up_xh, 1, gx_id(gx_dn))
+    up_y = remote(send_y, up_yh, 2, {"gy": gy_dn})
+
+    pl.semaphore_wait(barrier, len(greeted))
+
+    @pl.when(gz == 1)
+    def _():
+        up_z.start()
+        up_raw[...] = jnp.zeros(up_raw.shape, jnp.float32)
+
     for copy in smalls:
         copy.wait()
+
+    for device_id in beside(1):
+        signal(near, device_id)
 
     row16 = lax.broadcasted_iota(jnp.int32, (16, 128), 0)
     lane16 = lax.broadcasted_iota(jnp.int32, (16, 128), 1)
@@ -145,62 +165,102 @@
 
     lax.fori_loop(0, nz + 1, z_stretch, 0)
 
-    for c in range(2):
+    acc[...] = jnp.zeros(acc.shape, jnp.float32)
+    sym[...] = jnp.zeros(sym.shape, jnp.float32)
+    zero8 = jnp.zeros((8, 128), jnp.float32)
+
+    pltpu.make_async_copy(fields, v, load_sem).wait()
+
+    def combine(vr, vi, b):
+        re = im = None
         for a in range(NV):
-            for b in range(NV):
-                acc[c, a, b] = jnp.zeros((8, 128), jnp.float32)
-        for k in range(len(PAIRS)):
-            sym[c, k] = jnp.zeros((8, 128), jnp.float32)
-
-    def rotate(z, packed):
-        load(z).wait()
-        packed = list(packed)
+            cr, ci = coef[0, a, b], coef[1, a, b]
+            pr = cr * vr[a] - ci * vi[a]
+            pi = cr * vi[a] + ci * vr[a]
+            re = pr if re is None else re + pr
+            im = pi if im is None else im + pi
+        return re, im
+
+    def packed_lanes(ref, comp, lane):
+        tile = None
+        for c in range(2):
+            for a in range(NV):
+                part = None
+                for z in range(nz):
+                    for t in range(2):
+                        column = ref[c, a, comp, z, 8 * t : 8 * t + 8, lane : lane + 1]
+                        column = jnp.broadcast_to(column, (8, 128))
+                        place = 2 * z + t
+                        part = column if part is None else jnp.where(lane_in == place, column, part)
+                group = c * NV + a
+                tile = part if tile is None else jnp.where(lane_group == group, part, tile)
+        return tile
+
+    lane_in, lane_group = lane8 % 16, lane8 // 16
+    factors = []
+    for d in range(8):
+        factor = None
+        for out in range(8):
+            src = (out - d) % 8
+            a, b = src % NV, out % NV
+            if out // NV == src // NV:
+                value = coef[0, a, b]
+            elif out // NV == 0:
+                value = -coef[1, a, b]
+            else:
+                value = coef[1, a, b]
+            factor = (
+                jnp.full((8, 128), value, jnp.float32)
+                if factor is None
+                else jnp.where(lane_group == out, value, factor)
+            )
+        factors.append(factor)
+    for slot, comp in ((0, 0), (1, 2)):
+        raw = packed_lanes(v, comp, 0)
+        turned = factors[0] * raw
+        for d in range(1, 8):
+            turned = turned + factors[d] * pltpu.roll(raw, 16 * d, 1)
+        send_y[slot] = turned
+    up_y.start()
+
+    for comp in (1, 2):
+        rows = [
+            [
+                jnp.concatenate([v[c, a, comp, z, 0:1, :] for z in range(nz)], axis=0)
+                for a in range(NV)
+            ]
+            for c in range(2)
+        ]
+        for b in range(NV):
+            re, im = combine(rows[0], rows[1], b)
+            send_x[0, b, comp - 1] = re
+            send_x[1, b, comp - 1] = im
+    up_x.start()
+
+    def rotate(z, carry):
         for comp in range(3):
             vr = [v[0, a, comp, z] for a in range(NV)]
             vi = [v[1, a, comp, z] for a in range(NV)]
             for b in range(NV):
-                re = im = None
-                for a in range(NV):
-                    cr, ci = coef[0, a, b], coef[1, a, b]
-                    pr = cr * vr[a] - ci * vi[a]
-                    pi = cr * vi[a] + ci * vr[a]
-                    re = pr if re is None else re + pr
-                    im = pi if im is None else im + pi
-                for c, value in ((0, re), (1, im)):
-                    basis[c, b, comp, z] = value
-                    if comp != 0:
-                        send_x[c, b, comp - 1, pl.ds(z, 1), :] = value[0:1]
-                    if comp != 1:
-                        slot = comp // 2
-                        for t in range(2):
-                            place = (c * NV + b) * 16 + 2 * z + t
-                            first = jnp.broadcast_to(value[8 * t : 8 * t + 8, 0:1], (8, 128))
-                            packed[slot] = jnp.where(lane8 == place, first, packed[slot])
-        return tuple(packed)
-
-    zero8 = jnp.zeros((8, 128), jnp.float32)
-    packed = lax.fori_loop(0, nz, rotate, (zero8, zero8))
-    send_y[0] = packed[0]
-    send_y[1] = packed[1]
-
-    pl.semaphore_wait(barrier, greetings)
-
-    def remote(src, dst, slot, device_id):
-        return pltpu.make_async_remote_copy(
-            src_ref=src, dst_ref=dst, send_sem=halo_send.at[slot], recv_sem=halo_recv.at[slot],
-            device_id=device_id, device_id_type=MESH,
-        )
-
-    up_z = remote(basis.at[:, :, 0:2, 0], up_zh, 0, {"gz": 0})
-    up_x = remote(send_x, up_xh, 1, gx_id(gx_dn))
-    up_y = remote(send_y, up_yh, 2, {"gy": gy_dn})
-
-    @pl.when(gz == 1)
-    def _():
-        up_z.start()
-
-    up_x.start()
-    up_y.start()
+                re, im = combine(vr, vi, b)
+                basis[0, b, comp, z] = re
+                basis[1, b, comp, z] = im
+        return carry
+
+    lax.fori_loop(0, nz, rotate, 0)
+
+    def pair(ref, *index):
+        return ref[(0,) + index], ref[(1,) + index]
+
+    def three(value):
+        return value[0], value[1], value[0] + value[1]
+
+    def dot3(left, right):
+        sums = None
+        for p, q in zip(left, right):
+            terms = [x * y for x, y in zip(p, q)]
+            sums = terms if sums is None else [x + y for x, y in zip(sums, terms)]
+        return sums
 
     def local_gram(z, carry):
         m = mat[z]
@@ -213,19 +273,18 @@
         eps[0, z] = er
         eps[1, z] = ei
         for a in range(NV):
-            q = [cmul((er, ei), (basis[0, a, comp, z], basis[1, a, comp, z])) for comp in range(3)]
+            q = [three(cmul((er, ei), pair(basis, a, comp, z))) for comp in range(3)]
             for b in range(a, NV):
                 k = PAIRS.index((a, b))
-                re = im = None
-                for comp in range(3):
-                    pr, pi = cmul(q[comp], (basis[0, b, comp, z], basis[1, b, comp, z]))
-                    re = pr if re is None else re + pr
-                    im = pi if im is None else im + pi
-                sym[0, k] += fold(re)
-                sym[1, k] += fold(im)
+                for part, value in enumerate(dot3(q, [three(pair(basis, b, comp, z)) for comp in range(3)])):
+                    sym[part, k] += fold(value)
         return carry
 
     lax.fori_loop(0, nz, local_gram, 0)
+
+    pl.semaphore_wait(near, 4)
+    for device_id in beside(2):
+        signal(far, device_id)
 
     up_x.wait_recv()
     up_y.wait_recv()
@@ -237,9 +296,6 @@
     @pl.when(gy == n_gy - 1)
     def _():
         up_yh[...] = jnp.zeros(up_yh.shape, jnp.float32)
-
-    def pair(ref, *index):
-        return ref[(0,) + index], ref[(1,) + index]
 
     def stretch(kind):
         return sxy[kind, 0], sxy[kind, 1]
@@ -296,16 +352,14 @@
                             h[c, b, comp, z] = turned[comp][c]
                         else:
                             gs[c, b, comp] = turned[comp][c]
+                    if where == "g":
+                        gs[2, b, comp] = turned[comp][0] + turned[comp][1]
         for b in range(NV):
-            hb = [pair(h, b, comp, z) for comp in range(3)]
+            hb = [three(pair(h, b, comp, z)) for comp in range(3)]
             for a in range(NV):
-                re = im = None
-                for comp in range(3):
-                    pr, pi = cmul(pair(gs, a, comp), hb[comp])
-                    re = pr if re is None else re + pr
-                    im = pi if im is None else im + pi
-                acc[0, a, b] += fold(re)
-                acc[1, a, b] += fold(im)
+                ga = [(gs[0, a, comp], gs[1, a, comp], gs[2, a, comp]) for comp in range(3)]
+                for part, value in enumerate(dot3(ga, hb)):
+                    acc[part, a, b] += fold(value)
 
     def forward_step(z, carry):
         forward(z, lambda b, comp: pair(basis, b, comp, z + 1))
@@ -317,9 +371,11 @@
     def _():
         up_z.wait_recv()
 
-    @pl.when(gz == 1)
-    def _():
-        up_zh[...] = jnp.zeros(up_zh.shape, jnp.float32)
+    for comp in range(2):
+        vr = [up_raw[0, a, comp] for a in range(NV)]
+        vi = [up_raw[1, a, comp] for a in range(NV)]
+        for b in range(NV):
+            up_zh[0, b, comp], up_zh[1, b, comp] = combine(vr, vi, b)
 
     forward(nz - 1, lambda b, comp: pair(up_zh, b, comp))
 
@@ -328,65 +384,45 @@
         rows = zero8
         for c in range(2):
             for a in range(NV):
-                s = acc[c, a, b] - sym[c, PAIRS.index((min(a, b), max(a, b)))]
+                k = PAIRS.index((min(a, b), max(a, b)))
+                sums = [acc[part, a, b] - sym[part, k] for part in range(3)]
+                s = sums[0] - sums[1] if c == 0 else sums[2] - sums[0] - sums[1]
                 s = jnp.sum(s, axis=0, keepdims=True)
                 rows = jnp.where(row8 == c * NV + a, s, rows)
         total = jnp.sum(rows, axis=1, keepdims=True)
         tile = jnp.where(lane8 == b, total, tile)
 
     def exchange(buf, count, me, ids, ss, rs):
-        copies = []
         for d in range(1, count):
-            peer = (me + d) % count
-            copies.append(
-                pltpu.make_async_remote_copy(
-                    src_ref=buf.at[me], dst_ref=buf.at[me], send_sem=ss.at[d], recv_sem=rs.at[me],
-                    device_id=ids(peer), device_id_type=MESH,
-                )
-            )
-        for copy in copies:
-            copy.start()
+            pltpu.make_async_remote_copy(
+                src_ref=buf.at[me], dst_ref=buf.at[me], send_sem=ss, recv_sem=rs,
+                device_id=ids((me + d) % count), device_id_type=MESH,
+            ).start()
+        others = buf.at[pl.ds(0, count - 1)]
 
         def arrived():
-            for d in range(1, count):
-                peer = (me + d) % count
-                pltpu.make_async_remote_copy(
-                    src_ref=buf.at[peer], dst_ref=buf.at[peer], send_sem=ss.at[d],
-                    recv_sem=rs.at[peer], device_id=ids(peer), device_id_type=MESH,
-                ).wait_recv()
+            pltpu.make_async_copy(others, others, rs).wait()
             total = buf[0]
             for k in range(1, count):
                 total = total + buf[k]
             return total
 
         def sent():
-            for copy in copies:
-                copy.wait_send()
+            pltpu.make_async_copy(others, others, ss).wait()
 
         return arrived, sent
 
     buf1[g1] = tile
     arrived1, sent1 = exchange(buf1, n1, g1, g1_id, ss1, rs1)
 
-    def pack(z, packed):
-        packed = list(packed)
+    hsend_y[0] = packed_lanes(h, 0, 127)
+    hsend_y[1] = packed_lanes(h, 2, 127)
+    for c in range(2):
         for b in range(NV):
-            for c in range(2):
-                for comp in range(3):
-                    value = h[c, b, comp, z]
-                    if comp != 0:
-                        hsend_x[c, b, comp - 1, pl.ds(z, 1), :] = value[15:16]
-                    if comp != 1:
-                        slot = comp // 2
-                        for t in range(2):
-                            place = (c * NV + b) * 16 + 2 * z + t
-                            last = jnp.broadcast_to(value[8 * t : 8 * t + 8, 127:128], (8, 128))
-                            packed[slot] = jnp.where(lane8 == place, last, packed[slot])
-        return tuple(packed)
-
-    packed = lax.fori_loop(0, nz, pack, (zero8, zero8))
-    hsend_y[0] = packed[0]
-    hsend_y[1] = packed[1]
+            for comp in (1, 2):
+                hsend_x[c, b, comp - 1] = jnp.concatenate(
+                    [h[c, b, comp, z, 15:16, :] for z in range(nz)], axis=0
+                )
     dn_z = remote(h.at[:, :, 0:2, nz - 1], dn_zh, 3, {"gz": 1})
     dn_x = remote(hsend_x, dn_xh, 4, gx_id(gx_up))
     dn_y = remote(hsend_y, dn_yh, 5, {"gy": gy_up})
@@ -398,6 +434,7 @@
     dn_x.start()
     dn_y.start()
 
+    pl.semaphore_wait(far, 4)
     buf2[gy] = arrived1()
     arrived2, sent2 = exchange(buf2, n_gy, gy, lambda k: {"gy": k}, ss2, rs2)
 
@@ -483,6 +520,18 @@
     sent3()
 
 
+def write_out(basis, resid, gram, basis_out, resid_out, gram_out, sem):
+    copies = [pltpu.make_async_copy(gram, gram_out, sem.at[16])]
+    for k in range(8):
+        c, a = k // 4, k % 4
+        copies.append(pltpu.make_async_copy(basis.at[c, a], basis_out.at[c, a], sem.at[2 * k]))
+        copies.append(pltpu.make_async_copy(resid.at[c, a], resid_out.at[c, a], sem.at[2 * k + 1]))
+    for copy in copies:
+        copy.start()
+    for copy in copies:
+        copy.wait()
+
+
 def body(sizes, fields, material, pml_width, eps_real, eps_loss, coeffs, ritz):
     nz, nx, ny, n_gx, n_gy, n_gz, n_zz = sizes
     n1 = n_gx // n_zz * n_gz
@@ -493,7 +542,7 @@
     face_y = pltpu.VMEM((2, 8, 128), f32)
     face_z = pltpu.VMEM((2, NV, 2, nx, ny), f32)
     dma = pltpu.SemaphoreType.DMA
-    return pl.pallas_call(
+    made = pl.pallas_call(
         functools.partial(kernel, sizes),
         out_shape=(
             jax.ShapeDtypeStruct(whole, f32),
@@ -511,29 +560,38 @@
             pltpu.VMEM((nz, nx, ny), jnp.int32),
             pltpu.VMEM(whole, f32),
             pltpu.VMEM(whole, f32),
-            pltpu.VMEM((2, NV, 3, nx, ny), f32),
-            pltpu.VMEM((2, NV, NV, 8, 128), f32),
-            pltpu.VMEM((2, len(PAIRS), 8, 128), f32),
+            pltpu.VMEM((3, NV, 3, nx, ny), f32),
+            pltpu.VMEM((3, NV, NV, 8, 128), f32),
+            pltpu.VMEM((3, len(PAIRS), 8, 128), f32),
             pltpu.VMEM((2, nz, nx, ny), f32),
             pltpu.VMEM((6, 2, nx, ny), f32),
             pltpu.VMEM((2, 2, nz + 1, 8, 128), f32),
-            face_x, face_y, face_x, face_y, face_z,
+            face_x, face_y, face_x, face_y, face_z, face_z,
             face_x, face_y, face_x, face_y, face_z,
             pltpu.VMEM((n1, 8, 128), f32),
             pltpu.VMEM((n_gy, 8, 128), f32),
             pltpu.VMEM((n_zz, 8, 128), f32),
             dma((6,)),
-            dma((nz,)),
+            dma,
             dma((6,)),
             dma((6,)),
-            dma((n1,)), dma((n1,)),
-            dma((n_gy,)), dma((n_gy,)),
-            dma((n_zz,)), dma((n_zz,)),
+            dma, dma, dma, dma, dma, dma,
+            pltpu.SemaphoreType.REGULAR,
+            pltpu.SemaphoreType.REGULAR,
         ],
         compiler_params=pltpu.CompilerParams(
             collective_id=0, has_side_effects=True, vmem_limit_bytes=24 * 1024 * 1024
         ),
     )(*(pltpu.with_memory_space_constraint(x, pltpu.HBM) for x in (pml_width, eps_real, eps_loss, coeffs, ritz, material, fields)))
+    hbm = pl.BlockSpec(memory_space=pltpu.HBM)
+    return pl.pallas_call(
+        write_out,
+        out_shape=tuple(jax.ShapeDtypeStruct(x.shape, f32) for x in made),
+        in_specs=[vmem] * 3,
+        out_specs=(hbm,) * 3,
+        scratch_shapes=[dma((17,))],
+        compiler_params=pltpu.CompilerParams(vmem_limit_bytes=1024 * 1024),
+    )(*made)
 
 
 def solution(mesh):

time: 36.9 us -> 36 us (0.976)
  local copies, waits for them, and re-layouts: 2.88 us -> 0 us
  Pallas kernels: 33.3 us -> 35.2 us
    unnamed x3 -> x0, local copies, waits for them, and re-layouts: 2.88 us -> none
    pallas_call x0 -> x1, Pallas kernels: none -> 1.8 us  [body(): pl.pallas_call(write_out, out_shape=tuple((jax.ShapeDtypeStruct(x.shape,...]
where the time goes in v2:
time: 36 us; the launch traced here: 35.9 us
  Pallas kernels  35.2 us (98%)
  between operations  0.64 us (2%)
    pallas_call x1, Pallas kernels, body(): pl.pallas_call(functools.partial(kernel, sizes), out_shape=(jax.ShapeDtyp...  33.4 us
    pallas_call x1, Pallas kernels, body(): pl.pallas_call(write_out, out_shape=tuple((jax.ShapeDtypeStruct(x.shape,...  1.8 us

profile of v2, /device:TPU:1, one launch (start us, length us, event | category | flops | bytes accessed | tf_op | source)
XLA Modules:
  0.0 35.9 jit_solution(5287717867219954309)
XLA Ops:
  0.6 33.4 %shard_map.94 = (f32[2,4,3,8,16,128]{5,4,3,2,1,0:T(8,128)S(1)}, f32[2,4,3,8,16,128]{5,4,3,2,1,0:T(8,128)S(1)}, f32[2,4,4]{2,1,0:T(4,128)S(1)}) custom-call(s32[6]{0:T(128)} %pml_hbm.1, f32[4]{0:T(128)} %eps_r_hbm.1, f32[4]{0:T(128)} %eps_l_hbm.1, f32[2,4,4]{2,1,0:T(4,128)} %coef_hbm.1, f32[2,4]{1,0:T(2,128)} %ritz_hbm.1, s32[8,16,128]{2,1,0:T(8,128)} %mat_hbm.1, ...), custom_call_target="tpu_custom_call" | custom-call | tf_op jit(solution)/shard_map/pallas_call | solution.py:545
  34.1 1.8 %shard_map.95 = (f32[2,4,3,8,16,128]{5,4,3,2,1,0:T(8,128)}, f32[2,4,3,8,16,128]{5,4,3,2,1,0:T(8,128)}, f32[2,4,4]{2,1,0:T(4,128)}) custom-call(f32[2,4,3,8,16,128]{5,4,3,2,1,0:T(8,128)S(1)} %get-tuple-element.6.basis, f32[2,4,3,8,16,128]{5,4,3,2,1,0:T(8,128)S(1)} %get-tuple-element.7.resid, f32[2,4,4]{2,1,0:T(4,128)S(1)} %get-tuple-element.8.gram), custom_call_target="tpu_custom_call" | custom-call | tf_op jit(solution)/shard_map/pallas_call | solution.py:587

commit v3 on v2

--- a/solution.py
+++ b/solution.py
@@ -50,7 +50,7 @@
     pml_hbm, eps_r_hbm, eps_l_hbm, coef_hbm, ritz_hbm, mat_hbm, fields,
     basis, resid, gram,
     pml, eps_r, eps_l, coef, ritz, mat, v, h, gs, acc, sym, eps, sxy, sz,
-    send_x, send_y, up_xh, up_yh, up_raw, up_zh,
+    send_x, send_y, up_xh, up_yh, up_raw, layers,
     hsend_x, hsend_y, dn_xh, dn_yh, dn_zh,
     buf1, buf2, buf3,
     small_sem, load_sem, halo_send, halo_recv, ss1, rs1, ss2, rs2, ss3, rs3, near, far,
@@ -84,9 +84,11 @@
     for copy in smalls:
         copy.start()
 
-    for c in range(2):
-        for a in range(NV):
-            pltpu.make_async_copy(fields.at[c, a], v.at[c, a], load_sem).start()
+    for comp in (0, 2, 1):
+        for c in range(2):
+            pltpu.make_async_copy(
+                fields.at[c, :, comp], v.at[c, :, comp], load_sem.at[comp]
+            ).start()
 
     barrier = pltpu.get_barrier_semaphore()
 
@@ -169,34 +171,47 @@
     sym[...] = jnp.zeros(sym.shape, jnp.float32)
     zero8 = jnp.zeros((8, 128), jnp.float32)
 
-    pltpu.make_async_copy(fields, v, load_sem).wait()
-
-    def combine(vr, vi, b):
-        re = im = None
+    def loaded(comp):
+        pltpu.make_async_copy(fields.at[:, :, comp], v.at[:, :, comp], load_sem.at[comp]).wait()
+
+    def combine(vr, vi, vs, b):
+        both = minus = plus = None
         for a in range(NV):
             cr, ci = coef[0, a, b], coef[1, a, b]
-            pr = cr * vr[a] - ci * vi[a]
-            pi = cr * vi[a] + ci * vr[a]
-            re = pr if re is None else re + pr
-            im = pi if im is None else im + pi
-        return re, im
+            p, q, r = cr * vs[a], (ci - cr) * vr[a], (cr + ci) * vi[a]
+            both = p if both is None else both + p
+            minus = q if minus is None else minus + q
+            plus = r if plus is None else plus + r
+        return both - plus, both + minus
+
+    def combined(vr, vi):
+        vs = [x + y for x, y in zip(vr, vi)]
+        return [combine(vr, vi, vs, b) for b in range(NV)]
 
     def packed_lanes(ref, comp, lane):
-        tile = None
+        at = (lane8 + (128 - lane)) % 128
+
+        def merge(blocks, step):
+            half = len(blocks) // 2
+            keep = at % (2 * step) < step
+            return [
+                jnp.where(keep, blocks[k], pltpu.roll(blocks[k + half], step, 1)) for k in range(half)
+            ]
+
+        groups = []
         for c in range(2):
             for a in range(NV):
-                part = None
-                for z in range(nz):
-                    for t in range(2):
-                        column = ref[c, a, comp, z, 8 * t : 8 * t + 8, lane : lane + 1]
-                        column = jnp.broadcast_to(column, (8, 128))
-                        place = 2 * z + t
-                        part = column if part is None else jnp.where(lane_in == place, column, part)
-                group = c * NV + a
-                tile = part if tile is None else jnp.where(lane_group == group, part, tile)
-        return tile
-
-    lane_in, lane_group = lane8 % 16, lane8 // 16
+                blocks = [
+                    ref[c, a, comp, z, 8 * t : 8 * t + 8] for z in range(nz) for t in range(2)
+                ]
+                for step in (8, 4, 2, 1):
+                    blocks = merge(blocks, step)
+                groups += blocks
+        for step in (64, 32, 16):
+            groups = merge(groups, step)
+        return groups[0] if lane == 0 else pltpu.roll(groups[0], 128 - lane, 1)
+
+    lane_group = lane8 // 16
     factors = []
     for d in range(8):
         factor = None
@@ -216,6 +231,7 @@
             )
         factors.append(factor)
     for slot, comp in ((0, 0), (1, 2)):
+        loaded(comp)
         raw = packed_lanes(v, comp, 0)
         turned = factors[0] * raw
         for d in range(1, 8):
@@ -223,6 +239,7 @@
         send_y[slot] = turned
     up_y.start()
 
+    loaded(1)
     for comp in (1, 2):
         rows = [
             [
@@ -231,8 +248,7 @@
             ]
             for c in range(2)
         ]
-        for b in range(NV):
-            re, im = combine(rows[0], rows[1], b)
+        for b, (re, im) in enumerate(combined(*rows)):
             send_x[0, b, comp - 1] = re
             send_x[1, b, comp - 1] = im
     up_x.start()
@@ -241,10 +257,12 @@
         for comp in range(3):
             vr = [v[0, a, comp, z] for a in range(NV)]
             vi = [v[1, a, comp, z] for a in range(NV)]
-            for b in range(NV):
-                re, im = combine(vr, vi, b)
+            for b, (re, im) in enumerate(combined(vr, vi)):
                 basis[0, b, comp, z] = re
                 basis[1, b, comp, z] = im
+                if comp < 2:
+                    layers[0, b, comp, z] = re
+                    layers[1, b, comp, z] = im
         return carry
 
     lax.fori_loop(0, nz, rotate, 0)
@@ -297,6 +315,9 @@
     def _():
         up_yh[...] = jnp.zeros(up_yh.shape, jnp.float32)
 
+    def pair_z(kind, z):
+        return sz[kind, 0, z], sz[kind, 1, z]
+
     def stretch(kind):
         return sxy[kind, 0], sxy[kind, 1]
 
@@ -310,74 +331,110 @@
             parts.append(pltpu.roll(ref[slot], (lane - place) % 128, 1))
         return jnp.concatenate(parts, axis=0)
 
-    def forward(z, next_z):
+    def forward(z, t, on_x, on_y, on_z):
+        half = slice(8 * t, 8 * t + 8)
+        plain = not (on_x or on_y or on_z)
+
+        def stretches(base):
+            return [(sxy[base + k, 0, half], sxy[base + k, 1, half]) for k in range(3)]
+
+        sx = stretches(0) if on_x else None
+        sy = stretches(3) if on_y else None
+        sz3 = [pair_z(0, z), pair_z(1, z), pair_z(1, z + 1)] if on_z else None
         for b in range(NV):
-            f = [pair(basis, b, comp, z) for comp in range(3)]
-
-            def both(comp, ahead, sh, se, se_next):
+            f = [pair(basis, b, comp, z, half) for comp in range(3)]
+
+            def both(comp, ahead, factors3):
                 d = csub(ahead, f[comp])
+                if factors3 is None:
+                    return d, d
+                sh, se, se_next = factors3
                 return cmul(sh, d), csub(cmul(se_next, ahead), cmul(se, f[comp]))
 
             dx, dy, dz = {}, {}, {}
             for comp in (1, 2):
-                ahead = tuple(
-                    jnp.where(
-                        row16 == 15,
-                        up_xh[c, b, comp - 1, pl.ds(z, 1), :],
-                        pltpu.roll(f[comp][c], 15, 0),
-                    )
-                    for c in range(2)
-                )
-                dx[comp] = both(comp, ahead, stretch(0), stretch(1), stretch(2))
+                ahead = []
+                for c in range(2):
+                    if t == 0:
+                        edge = basis[c, b, comp, z, 8:9]
+                    else:
+                        edge = up_xh[c, b, comp - 1, pl.ds(z, 1), :]
+                    ahead.append(jnp.where(row8 == 7, edge, pltpu.roll(f[comp][c], 7, 0)))
+                dx[comp] = both(comp, ahead, sx)
             for comp in (0, 2):
-                ahead = tuple(
-                    jnp.where(
-                        lane16 == 127,
-                        unpacked(up_yh, comp // 2, c, b, z, 127),
-                        pltpu.roll(f[comp][c], 127, 1),
-                    )
-                    for c in range(2)
-                )
-                dy[comp] = both(comp, ahead, stretch(3), stretch(4), stretch(5))
+                ahead = []
+                for c in range(2):
+                    place = (c * NV + b) * 16 + 2 * z + t
+                    edge = pltpu.roll(up_yh[comp // 2], 127 - place, 1)
+                    ahead.append(jnp.where(lane8 == 127, edge, pltpu.roll(f[comp][c], 127, 1)))
+                dy[comp] = both(comp, ahead, sy)
             for comp in (0, 1):
-                ahead = next_z(b, comp)
-                dz[comp] = both(
-                    comp, ahead, stretch_z(0, z), stretch_z(1, z), stretch_z(1, z + 1)
-                )
-            for part, where in ((0, "h"), (1, "g")):
-                turned = curl(*({k: t[part] for k, t in d.items()} for d in (dx, dy, dz)))
+                dz[comp] = both(comp, pair(layers, b, comp, z + 1, half), sz3)
+            turned = curl(*({k: x[0] for k, x in d.items()} for d in (dx, dy, dz)))
+            for comp in range(3):
+                for c in range(2):
+                    h[c, b, comp, z, half] = turned[comp][c]
+            if not plain:
+                turned = curl(*({k: x[1] for k, x in d.items()} for d in (dx, dy, dz)))
                 for comp in range(3):
-                    for c in range(2):
-                        if where == "h":
-                            h[c, b, comp, z] = turned[comp][c]
-                        else:
-                            gs[c, b, comp] = turned[comp][c]
-                    if where == "g":
-                        gs[2, b, comp] = turned[comp][0] + turned[comp][1]
+                    for c, value in enumerate(three(turned[comp])):
+                        gs[c, b, comp] = value
         for b in range(NV):
-            hb = [three(pair(h, b, comp, z)) for comp in range(3)]
-            for a in range(NV):
-                ga = [(gs[0, a, comp], gs[1, a, comp], gs[2, a, comp]) for comp in range(3)]
+            hb = [three(pair(h, b, comp, z, half)) for comp in range(3)]
+            for a in range(b + 1 if plain else NV):
+                if plain:
+                    ga = [three(pair(h, a, comp, z, half)) for comp in range(3)]
+                else:
+                    ga = [(gs[0, a, comp], gs[1, a, comp], gs[2, a, comp]) for comp in range(3)]
                 for part, value in enumerate(dot3(ga, hb)):
-                    acc[part, a, b] += fold(value)
-
-    def forward_step(z, carry):
-        forward(z, lambda b, comp: pair(basis, b, comp, z + 1))
+                    if plain:
+                        sym[part, PAIRS.index((a, b))] -= value
+                    else:
+                        acc[part, a, b] += value
+
+    y_edge = jnp.logical_or(gy == 0, gy == n_gy - 1)
+    last = nz - 1
+
+    def sweep(phase, carry):
+        @pl.when(phase == 1)
+        def _():
+            @pl.when(gz == 0)
+            def _():
+                up_z.wait_recv()
+
+            for comp in range(2):
+                vr = [up_raw[0, a, comp] for a in range(NV)]
+                vi = [up_raw[1, a, comp] for a in range(NV)]
+                for b, (re, im) in enumerate(combined(vr, vi)):
+                    layers[0, b, comp, nz] = re
+                    layers[1, b, comp, nz] = im
+
+        on_lo = (1 - phase) * ((nz - 5) * gz) + phase * last
+        on_hi = (1 - phase) * (4 + (nz - 5) * gz) + phase * (last + gz)
+        off_lo = (1 - phase) * (4 * (1 - gz)) + phase * last
+        off_hi = (1 - phase) * (last - 4 * gz) + phase * (nz - gz)
+
+        def layers_of(t, on_x, on_y):
+            for on_z, lo, hi in ((True, on_lo, on_hi), (False, off_lo, off_hi)):
+                def step(z, inner, on_z=on_z):
+                    forward(z, t, on_x, on_y, on_z)
+                    return inner
+
+                lax.fori_loop(lo, hi, step, 0)
+
+        for on_y in (False, True):
+            @pl.when(y_edge == on_y)
+            def _():
+                for t in range(2):
+                    x_edge = gx == (0 if t == 0 else n_gx - 1)
+                    for on_x in (False, True):
+                        @pl.when(x_edge == on_x)
+                        def _():
+                            layers_of(t, on_x, on_y)
+
         return carry
 
-    lax.fori_loop(0, nz - 1, forward_step, 0)
-
-    @pl.when(gz == 0)
-    def _():
-        up_z.wait_recv()
-
-    for comp in range(2):
-        vr = [up_raw[0, a, comp] for a in range(NV)]
-        vi = [up_raw[1, a, comp] for a in range(NV)]
-        for b in range(NV):
-            up_zh[0, b, comp], up_zh[1, b, comp] = combine(vr, vi, b)
-
-    forward(nz - 1, lambda b, comp: pair(up_zh, b, comp))
+    lax.fori_loop(0, 2, sweep, 0)
 
     tile = zero8
     for b in range(NV):
@@ -560,19 +617,20 @@
             pltpu.VMEM((nz, nx, ny), jnp.int32),
             pltpu.VMEM(whole, f32),
             pltpu.VMEM(whole, f32),
-            pltpu.VMEM((3, NV, 3, nx, ny), f32),
+            pltpu.VMEM((3, NV, 3, 8, 128), f32),
             pltpu.VMEM((3, NV, NV, 8, 128), f32),
             pltpu.VMEM((3, len(PAIRS), 8, 128), f32),
             pltpu.VMEM((2, nz, nx, ny), f32),
             pltpu.VMEM((6, 2, nx, ny), f32),
             pltpu.VMEM((2, 2, nz + 1, 8, 128), f32),
-            face_x, face_y, face_x, face_y, face_z, face_z,
+            face_x, face_y, face_x, face_y, face_z,
+            pltpu.VMEM((2, NV, 2, nz + 1, nx, ny), f32),
             face_x, face_y, face_x, face_y, face_z,
             pltpu.VMEM((n1, 8, 128), f32),
             pltpu.VMEM((n_gy, 8, 128), f32),
             pltpu.VMEM((n_zz, 8, 128), f32),
             dma((6,)),
-            dma,
+            dma((3,)),
             dma((6,)),
             dma((6,)),
             dma, dma, dma, dma, dma, dma,

time: 36 us -> 36.3 us (level)
  Pallas kernels: 35.2 us -> 35.6 us
where the time goes in v3:
time: 36.3 us; the launch traced here: 36.2 us
  Pallas kernels  35.6 us (98%)
  between operations  0.64 us (2%)
    pallas_call x1, Pallas kernels, body(): pl.pallas_call(functools.partial(kernel, sizes), out_shape=(jax.ShapeDtyp...  33.8 us
    pallas_call x1, Pallas kernels, body(): pl.pallas_call(write_out, out_shape=tuple((jax.ShapeDtypeStruct(x.shape,...  1.8 us

profile of v3, /device:TPU:1, one launch (start us, length us, event | category | flops | bytes accessed | tf_op | source)
XLA Modules:
  0.0 36.2 jit_solution(2793341704470398165)
XLA Ops:
  0.6 33.8 %shard_map.94 = (f32[2,4,3,8,16,128]{5,4,3,2,1,0:T(8,128)S(1)}, f32[2,4,3,8,16,128]{5,4,3,2,1,0:T(8,128)S(1)}, f32[2,4,4]{2,1,0:T(4,128)S(1)}) custom-call(s32[6]{0:T(128)} %pml_hbm.1, f32[4]{0:T(128)} %eps_r_hbm.1, f32[4]{0:T(128)} %eps_l_hbm.1, f32[2,4,4]{2,1,0:T(4,128)} %coef_hbm.1, f32[2,4]{1,0:T(2,128)} %ritz_hbm.1, s32[8,16,128]{2,1,0:T(8,128)} %mat_hbm.1, ...), custom_call_target="tpu_custom_call" | custom-call | tf_op jit(solution)/shard_map/pallas_call | solution.py:602
  34.4 1.8 %shard_map.95 = (f32[2,4,3,8,16,128]{5,4,3,2,1,0:T(8,128)}, f32[2,4,3,8,16,128]{5,4,3,2,1,0:T(8,128)}, f32[2,4,4]{2,1,0:T(4,128)}) custom-call(f32[2,4,3,8,16,128]{5,4,3,2,1,0:T(8,128)S(1)} %get-tuple-element.6.basis, f32[2,4,3,8,16,128]{5,4,3,2,1,0:T(8,128)S(1)} %get-tuple-element.7.resid, f32[2,4,4]{2,1,0:T(4,128)S(1)} %get-tuple-element.8.gram), custom_call_target="tpu_custom_call" | custom-call | tf_op jit(solution)/shard_map/pallas_call | solution.py:645

commit v4 on v3

--- a/solution.py
+++ b/solution.py
@@ -189,29 +189,21 @@
         return [combine(vr, vi, vs, b) for b in range(NV)]
 
     def packed_lanes(ref, comp, lane):
-        at = (lane8 + (128 - lane)) % 128
-
-        def merge(blocks, step):
-            half = len(blocks) // 2
-            keep = at % (2 * step) < step
-            return [
-                jnp.where(keep, blocks[k], pltpu.roll(blocks[k + half], step, 1)) for k in range(half)
-            ]
-
-        groups = []
+        tile = None
         for c in range(2):
             for a in range(NV):
-                blocks = [
-                    ref[c, a, comp, z, 8 * t : 8 * t + 8] for z in range(nz) for t in range(2)
-                ]
-                for step in (8, 4, 2, 1):
-                    blocks = merge(blocks, step)
-                groups += blocks
-        for step in (64, 32, 16):
-            groups = merge(groups, step)
-        return groups[0] if lane == 0 else pltpu.roll(groups[0], 128 - lane, 1)
-
-    lane_group = lane8 // 16
+                part = None
+                for z in range(nz):
+                    for t in range(2):
+                        column = ref[c, a, comp, z, 8 * t : 8 * t + 8, lane : lane + 1]
+                        column = jnp.broadcast_to(column, (8, 128))
+                        place = 2 * z + t
+                        part = column if part is None else jnp.where(lane_in == place, column, part)
+                group = c * NV + a
+                tile = part if tile is None else jnp.where(lane_group == group, part, tile)
+        return tile
+
+    lane_in, lane_group = lane8 % 16, lane8 // 16
     factors = []
     for d in range(8):
         factor = None
@@ -315,9 +307,6 @@
     def _():
         up_yh[...] = jnp.zeros(up_yh.shape, jnp.float32)
 
-    def pair_z(kind, z):
-        return sz[kind, 0, z], sz[kind, 1, z]
-
     def stretch(kind):
         return sxy[kind, 0], sxy[kind, 1]
 
@@ -331,68 +320,77 @@
             parts.append(pltpu.roll(ref[slot], (lane - place) % 128, 1))
         return jnp.concatenate(parts, axis=0)
 
-    def forward(z, t, on_x, on_y, on_z):
-        half = slice(8 * t, 8 * t + 8)
+    def forward(z, on_x, on_y, on_z):
         plain = not (on_x or on_y or on_z)
-
-        def stretches(base):
-            return [(sxy[base + k, 0, half], sxy[base + k, 1, half]) for k in range(3)]
-
-        sx = stretches(0) if on_x else None
-        sy = stretches(3) if on_y else None
-        sz3 = [pair_z(0, z), pair_z(1, z), pair_z(1, z + 1)] if on_z else None
+        sx = [stretch(k) for k in range(3)] if on_x else None
+        sy = [stretch(3 + k) for k in range(3)] if on_y else None
+        sz3 = [stretch_z(0, z), stretch_z(1, z), stretch_z(1, z + 1)] if on_z else None
         for b in range(NV):
-            f = [pair(basis, b, comp, z, half) for comp in range(3)]
-
-            def both(comp, ahead, factors3):
+            f = [pair(basis, b, comp, z) for comp in range(3)]
+
+            def both(comp, ahead, factors3, upper=False):
                 d = csub(ahead, f[comp])
                 if factors3 is None:
                     return d, d
-                sh, se, se_next = factors3
-                return cmul(sh, d), csub(cmul(se_next, ahead), cmul(se, f[comp]))
+                rows = slice(8, 16) if upper else slice(0, 16)
+                part = lambda value: [x[rows] for x in value]
+                sh, se, se_next = (part(x) for x in factors3)
+                near_part, far_part = part(f[comp]), part(ahead)
+                results = cmul(sh, part(d)), csub(cmul(se_next, far_part), cmul(se, near_part))
+                if not upper:
+                    return results
+                return tuple(
+                    [jnp.concatenate([d[c][0:8], value[c]], axis=0) for c in range(2)]
+                    for value in results
+                )
 
             dx, dy, dz = {}, {}, {}
             for comp in (1, 2):
-                ahead = []
-                for c in range(2):
-                    if t == 0:
-                        edge = basis[c, b, comp, z, 8:9]
-                    else:
-                        edge = up_xh[c, b, comp - 1, pl.ds(z, 1), :]
-                    ahead.append(jnp.where(row8 == 7, edge, pltpu.roll(f[comp][c], 7, 0)))
-                dx[comp] = both(comp, ahead, sx)
+                ahead = [
+                    jnp.where(
+                        row16 == 15,
+                        up_xh[c, b, comp - 1, pl.ds(z, 1), :],
+                        pltpu.roll(f[comp][c], 15, 0),
+                    )
+                    for c in range(2)
+                ]
+                dx[comp] = both(comp, ahead, sx, on_x == "upper")
             for comp in (0, 2):
-                ahead = []
-                for c in range(2):
-                    place = (c * NV + b) * 16 + 2 * z + t
-                    edge = pltpu.roll(up_yh[comp // 2], 127 - place, 1)
-                    ahead.append(jnp.where(lane8 == 127, edge, pltpu.roll(f[comp][c], 127, 1)))
+                ahead = [
+                    jnp.where(
+                        lane16 == 127,
+                        unpacked(up_yh, comp // 2, c, b, z, 127),
+                        pltpu.roll(f[comp][c], 127, 1),
+                    )
+                    for c in range(2)
+                ]
                 dy[comp] = both(comp, ahead, sy)
             for comp in (0, 1):
-                dz[comp] = both(comp, pair(layers, b, comp, z + 1, half), sz3)
+                dz[comp] = both(comp, pair(layers, b, comp, z + 1), sz3)
             turned = curl(*({k: x[0] for k, x in d.items()} for d in (dx, dy, dz)))
             for comp in range(3):
                 for c in range(2):
-                    h[c, b, comp, z, half] = turned[comp][c]
+                    h[c, b, comp, z] = turned[comp][c]
             if not plain:
                 turned = curl(*({k: x[1] for k, x in d.items()} for d in (dx, dy, dz)))
                 for comp in range(3):
                     for c, value in enumerate(three(turned[comp])):
                         gs[c, b, comp] = value
         for b in range(NV):
-            hb = [three(pair(h, b, comp, z, half)) for comp in range(3)]
+            hb = [three(pair(h, b, comp, z)) for comp in range(3)]
             for a in range(b + 1 if plain else NV):
                 if plain:
-                    ga = [three(pair(h, a, comp, z, half)) for comp in range(3)]
+                    ga = [three(pair(h, a, comp, z)) for comp in range(3)]
                 else:
                     ga = [(gs[0, a, comp], gs[1, a, comp], gs[2, a, comp]) for comp in range(3)]
                 for part, value in enumerate(dot3(ga, hb)):
                     if plain:
-                        sym[part, PAIRS.index((a, b))] -= value
+                        sym[part, PAIRS.index((a, b))] -= fold(value)
                     else:
-                        acc[part, a, b] += value
-
-    y_edge = jnp.logical_or(gy == 0, gy == n_gy - 1)
+                        acc[part, a, b] += fold(value)
+
+    edge = jnp.logical_or(jnp.logical_or(gy == 0, gy == n_gy - 1), gx == 0)
+    x_end = gx == n_gx - 1
     last = nz - 1
 
     def sweep(phase, carry):
@@ -414,23 +412,24 @@
         off_lo = (1 - phase) * (4 * (1 - gz)) + phase * last
         off_hi = (1 - phase) * (last - 4 * gz) + phase * (nz - gz)
 
-        def layers_of(t, on_x, on_y):
-            for on_z, lo, hi in ((True, on_lo, on_hi), (False, off_lo, off_hi)):
-                def step(z, inner, on_z=on_z):
-                    forward(z, t, on_x, on_y, on_z)
-                    return inner
-
-                lax.fori_loop(lo, hi, step, 0)
-
-        for on_y in (False, True):
-            @pl.when(y_edge == on_y)
-            def _():
-                for t in range(2):
-                    x_edge = gx == (0 if t == 0 else n_gx - 1)
-                    for on_x in (False, True):
-                        @pl.when(x_edge == on_x)
-                        def _():
-                            layers_of(t, on_x, on_y)
+        def run(lo, hi, *flags):
+            def step(z, inner):
+                forward(z, *flags)
+                return inner
+
+            lax.fori_loop(lo, hi, step, 0)
+
+        @pl.when(edge)
+        def _():
+            run(phase * last, last + phase, "all", True, True)
+
+        @pl.when(jnp.logical_not(edge))
+        def _():
+            for at_end, on_x in ((False, None), (True, "upper")):
+                @pl.when(x_end == at_end)
+                def _():
+                    run(on_lo, on_hi, on_x, False, True)
+                    run(off_lo, off_hi, on_x, False, False)
 
         return carry
 
@@ -617,7 +616,7 @@
             pltpu.VMEM((nz, nx, ny), jnp.int32),
             pltpu.VMEM(whole, f32),
             pltpu.VMEM(whole, f32),
-            pltpu.VMEM((3, NV, 3, 8, 128), f32),
+            pltpu.VMEM((3, NV, 3, nx, ny), f32),
             pltpu.VMEM((3, NV, NV, 8, 128), f32),
             pltpu.VMEM((3, len(PAIRS), 8, 128), f32),
             pltpu.VMEM((2, nz, nx, ny), f32),

time: 36.3 us -> 35.4 us (0.975)
  Pallas kernels: 35.6 us -> 34.6 us
    pallas_call x1, Pallas kernels: 33.8 us -> 32.8 us  [body(): pl.pallas_call(functools.partial(kernel, sizes), out_shape=(jax.ShapeDtyp...]
where the time goes in v4:
time: 35.4 us; the launch traced here: 35.3 us
  Pallas kernels  34.6 us (98%)
  between operations  0.64 us (2%)
    pallas_call x1, Pallas kernels, body(): pl.pallas_call(functools.partial(kernel, sizes), out_shape=(jax.ShapeDtyp...  32.8 us
    pallas_call x1, Pallas kernels, body(): pl.pallas_call(write_out, out_shape=tuple((jax.ShapeDtypeStruct(x.shape,...  1.8 us

profile of v4, /device:TPU:1, one launch (start us, length us, event | category | flops | bytes accessed | tf_op | source)
XLA Modules:
  0.0 35.3 jit_solution(13747198357084406361)
XLA Ops:
  0.6 32.8 %shard_map.94 = (f32[2,4,3,8,16,128]{5,4,3,2,1,0:T(8,128)S(1)}, f32[2,4,3,8,16,128]{5,4,3,2,1,0:T(8,128)S(1)}, f32[2,4,4]{2,1,0:T(4,128)S(1)}) custom-call(s32[6]{0:T(128)} %pml_hbm.1, f32[4]{0:T(128)} %eps_r_hbm.1, f32[4]{0:T(128)} %eps_l_hbm.1, f32[2,4,4]{2,1,0:T(4,128)} %coef_hbm.1, f32[2,4]{1,0:T(2,128)} %ritz_hbm.1, s32[8,16,128]{2,1,0:T(8,128)} %mat_hbm.1, ...), custom_call_target="tpu_custom_call" | custom-call | tf_op jit(solution)/shard_map/pallas_call | solution.py:601
  33.5 1.8 %shard_map.95 = (f32[2,4,3,8,16,128]{5,4,3,2,1,0:T(8,128)}, f32[2,4,3,8,16,128]{5,4,3,2,1,0:T(8,128)}, f32[2,4,4]{2,1,0:T(4,128)}) custom-call(f32[2,4,3,8,16,128]{5,4,3,2,1,0:T(8,128)S(1)} %get-tuple-element.6.basis, f32[2,4,3,8,16,128]{5,4,3,2,1,0:T(8,128)S(1)} %get-tuple-element.7.resid, f32[2,4,4]{2,1,0:T(4,128)S(1)} %get-tuple-element.8.gram), custom_call_target="tpu_custom_call" | custom-call | tf_op jit(solution)/shard_map/pallas_call | solution.py:644

commit v5 on v4

--- a/solution.py
+++ b/solution.py
@@ -52,8 +52,8 @@
     pml, eps_r, eps_l, coef, ritz, mat, v, h, gs, acc, sym, eps, sxy, sz,
     send_x, send_y, up_xh, up_yh, up_raw, layers,
     hsend_x, hsend_y, dn_xh, dn_yh, dn_zh,
-    buf1, buf2, buf3,
-    small_sem, load_sem, halo_send, halo_recv, ss1, rs1, ss2, rs2, ss3, rs3, near, far,
+    buf1, buf2,
+    small_sem, load_sem, halo_send, halo_recv, ss1, rs1, ss2, rs2, near, far, opposite,
 ):
     nz, nx, ny, n_gx, n_gy, n_gz, n_zz = sizes
     n_x = n_gx // (2 * n_zz)
@@ -298,6 +298,9 @@
 
     up_x.wait_recv()
     up_y.wait_recv()
+    pl.semaphore_wait(far, 4)
+    for device_id in (beside(4)[0], beside(4)[2]):
+        signal(opposite, device_id)
 
     @pl.when(gx == n_gx - 1)
     def _():
@@ -446,10 +449,11 @@
                 s = jnp.sum(s, axis=0, keepdims=True)
                 rows = jnp.where(row8 == c * NV + a, s, rows)
         total = jnp.sum(rows, axis=1, keepdims=True)
-        tile = jnp.where(lane8 == b, total, tile)
+        tile = jnp.where(lane8 == NV * row8 + b, total, tile)
+    tile = jnp.sum(tile, axis=0, keepdims=True)
 
     def exchange(buf, count, me, ids, ss, rs):
-        for d in range(1, count):
+        for d in sorted(range(1, count), key=lambda d: abs(d - count // 2)):
             pltpu.make_async_remote_copy(
                 src_ref=buf.at[me], dst_ref=buf.at[me], send_sem=ss, recv_sem=rs,
                 device_id=ids((me + d) % count), device_id_type=MESH,
@@ -458,10 +462,10 @@
 
         def arrived():
             pltpu.make_async_copy(others, others, rs).wait()
-            total = buf[0]
-            for k in range(1, count):
-                total = total + buf[k]
-            return total
+            parts = [buf[k] for k in range(count)]
+            while len(parts) > 1:
+                parts = [parts[k] + parts[k + 1] for k in range(0, len(parts), 2)]
+            return parts[0]
 
         def sent():
             pltpu.make_async_copy(others, others, ss).wait()
@@ -490,9 +494,12 @@
     dn_x.start()
     dn_y.start()
 
-    pl.semaphore_wait(far, 4)
-    buf2[gy] = arrived1()
-    arrived2, sent2 = exchange(buf2, n_gy, gy, lambda k: {"gy": k}, ss2, rs2)
+    pl.semaphore_wait(opposite, 2)
+    plane = n_gy * n_zz
+    buf2[gy * n_zz + zz] = arrived1()
+    arrived2, sent2 = exchange(
+        buf2, plane, gy * n_zz + zz, lambda k: {"gy": k // n_zz, "zz": k % n_zz}, ss2, rs2
+    )
 
     dn_x.wait_recv()
     dn_y.wait_recv()
@@ -555,9 +562,6 @@
 
     lax.fori_loop(1, nz, backward_step, 0)
 
-    buf3[zz] = arrived2()
-    arrived3, sent3 = exchange(buf3, n_zz, zz, lambda k: {"zz": k}, ss3, rs3)
-
     @pl.when(gz == 1)
     def _():
         up_z.wait_send()
@@ -569,11 +573,14 @@
     for copy in (up_x, up_y, dn_x, dn_y):
         copy.wait_send()
     sent1()
+    final = arrived2() * (1.0 / (3.0 * total_x * total_y * total_z))
+    final = jnp.broadcast_to(final, (8, 128))
+    spread = final
+    for r in range(1, 2 * NV):
+        spread = jnp.where(row8 == r, pltpu.roll(final, 128 - NV * r, 1), spread)
+    gram[0] = spread[0:NV, 0:NV]
+    gram[1] = spread[NV : 2 * NV, 0:NV]
     sent2()
-    final = arrived3() * (1.0 / (3.0 * total_x * total_y * total_z))
-    gram[0] = final[0:NV, 0:NV]
-    gram[1] = final[NV : 2 * NV, 0:NV]
-    sent3()
 
 
 def write_out(basis, resid, gram, basis_out, resid_out, gram_out, sem):
@@ -625,14 +632,14 @@
             face_x, face_y, face_x, face_y, face_z,
             pltpu.VMEM((2, NV, 2, nz + 1, nx, ny), f32),
             face_x, face_y, face_x, face_y, face_z,
-            pltpu.VMEM((n1, 8, 128), f32),
-            pltpu.VMEM((n_gy, 8, 128), f32),
-            pltpu.VMEM((n_zz, 8, 128), f32),
+            pltpu.VMEM((n1, 1, 128), f32),
+            pltpu.VMEM((n_gy * n_zz, 1, 128), f32),
             dma((6,)),
             dma((3,)),
             dma((6,)),
             dma((6,)),
-            dma, dma, dma, dma, dma, dma,
+            dma, dma, dma, dma,
+            pltpu.SemaphoreType.REGULAR,
             pltpu.SemaphoreType.REGULAR,
             pltpu.SemaphoreType.REGULAR,
         ],

time: 35.4 us -> 33.5 us (0.946)
  Pallas kernels: 34.6 us -> 32.7 us
    pallas_call x1, Pallas kernels: 32.8 us -> 31 us  [body(): pl.pallas_call(functools.partial(kernel, sizes), out_shape=(jax.ShapeDtyp...]
where the time goes in v5:
time: 33.5 us; the launch traced here: 33.4 us
  Pallas kernels  32.7 us (98%)
  between operations  0.64 us (2%)
    pallas_call x1, Pallas kernels, body(): pl.pallas_call(functools.partial(kernel, sizes), out_shape=(jax.ShapeDtyp...  31 us
    pallas_call x1, Pallas kernels, body(): pl.pallas_call(write_out, out_shape=tuple((jax.ShapeDtypeStruct(x.shape,...  1.8 us

profile of v5, /device:TPU:1, one launch (start us, length us, event | category | flops | bytes accessed | tf_op | source)
XLA Modules:
  0.0 33.4 jit_solution(7047876145125332634)
XLA Ops:
  0.6 31.0 %shard_map.94 = (f32[2,4,3,8,16,128]{5,4,3,2,1,0:T(8,128)S(1)}, f32[2,4,3,8,16,128]{5,4,3,2,1,0:T(8,128)S(1)}, f32[2,4,4]{2,1,0:T(4,128)S(1)}) custom-call(s32[6]{0:T(128)} %pml_hbm.1, f32[4]{0:T(128)} %eps_r_hbm.1, f32[4]{0:T(128)} %eps_l_hbm.1, f32[2,4,4]{2,1,0:T(4,128)} %coef_hbm.1, f32[2,4]{1,0:T(2,128)} %ritz_hbm.1, s32[8,16,128]{2,1,0:T(8,128)} %mat_hbm.1, ...), custom_call_target="tpu_custom_call" | custom-call | tf_op jit(solution)/shard_map/pallas_call | solution.py:608
  31.6 1.8 %shard_map.95 = (f32[2,4,3,8,16,128]{5,4,3,2,1,0:T(8,128)}, f32[2,4,3,8,16,128]{5,4,3,2,1,0:T(8,128)}, f32[2,4,4]{2,1,0:T(4,128)}) custom-call(f32[2,4,3,8,16,128]{5,4,3,2,1,0:T(8,128)S(1)} %get-tuple-element.6.basis, f32[2,4,3,8,16,128]{5,4,3,2,1,0:T(8,128)S(1)} %get-tuple-element.7.resid, f32[2,4,4]{2,1,0:T(4,128)S(1)} %get-tuple-element.8.gram), custom_call_target="tpu_custom_call" | custom-call | tf_op jit(solution)/shard_map/pallas_call | solution.py:651

commit v6 on v5

--- a/solution.py
+++ b/solution.py
@@ -64,13 +64,21 @@
     g1 = (xh * n_gz + gz) * 2 + core
 
     def gx_id(index):
-        return {"xh": index // (2 * n_zz), "zz": (index // 2) % n_zz, "core": index % 2}
+        return {
+            "xh": lax.div(index, 2 * n_zz),
+            "zz": lax.rem(lax.div(index, 2), n_zz),
+            "core": lax.rem(index, 2),
+        }
 
     def g1_id(index):
-        return {"xh": index // (2 * n_gz), "gz": (index // 2) % n_gz, "core": index % 2}
-
-    gx_up, gx_dn = (gx + 1) % n_gx, (gx + n_gx - 1) % n_gx
-    gy_up, gy_dn = (gy + 1) % n_gy, (gy + n_gy - 1) % n_gy
+        return {
+            "xh": lax.div(index, 2 * n_gz),
+            "gz": lax.rem(lax.div(index, 2), n_gz),
+            "core": lax.rem(index, 2),
+        }
+
+    gx_up, gx_dn = lax.rem(gx + 1, n_gx), lax.rem(gx + n_gx - 1, n_gx)
+    gy_up, gy_dn = lax.rem(gy + 1, n_gy), lax.rem(gy + n_gy - 1, n_gy)
 
     smalls = [
         pltpu.make_async_copy(src, dst, small_sem.at[k])
@@ -97,14 +105,14 @@
 
     def beside(step):
         return (
-            {"gy": (gy + step) % n_gy},
-            {"gy": (gy + n_gy - step) % n_gy},
-            {"zz": (zz + step) % n_zz},
-            {"zz": (zz + n_zz - step) % n_zz},
+            {"gy": lax.rem(gy + step, n_gy)},
+            {"gy": lax.rem(gy + n_gy - step, n_gy)},
+            {"zz": lax.rem(zz + step, n_zz)},
+            {"zz": lax.rem(zz + n_zz - step, n_zz)},
         )
 
     greeted = [gx_id(gx_up), gx_id(gx_dn)] + list(beside(1))
-    greeted += [g1_id((g1 + d) % n1) for d in range(1, n1)]
+    greeted += [g1_id(lax.rem(g1 + d, n1)) for d in range(1, n1)]
     for device_id in greeted:
         signal(barrier, device_id)
 
@@ -259,6 +267,10 @@
 
     lax.fori_loop(0, nz, rotate, 0)
 
+    pl.semaphore_wait(near, 4)
+    for device_id in beside(2):
+        signal(far, device_id)
+
     def pair(ref, *index):
         return ref[(0,) + index], ref[(1,) + index]
 
@@ -292,15 +304,9 @@
 
     lax.fori_loop(0, nz, local_gram, 0)
 
-    pl.semaphore_wait(near, 4)
-    for device_id in beside(2):
-        signal(far, device_id)
 
     up_x.wait_recv()
     up_y.wait_recv()
-    pl.semaphore_wait(far, 4)
-    for device_id in (beside(4)[0], beside(4)[2]):
-        signal(opposite, device_id)
 
     @pl.when(gx == n_gx - 1)
     def _():
@@ -399,6 +405,10 @@
     def sweep(phase, carry):
         @pl.when(phase == 1)
         def _():
+            pl.semaphore_wait(far, 4)
+            for device_id in (beside(4)[0], beside(4)[2]):
+                signal(opposite, device_id)
+
             @pl.when(gz == 0)
             def _():
                 up_z.wait_recv()
@@ -453,10 +463,10 @@
     tile = jnp.sum(tile, axis=0, keepdims=True)
 
     def exchange(buf, count, me, ids, ss, rs):
-        for d in sorted(range(1, count), key=lambda d: abs(d - count // 2)):
+        for k in range(count - 1):
             pltpu.make_async_remote_copy(
                 src_ref=buf.at[me], dst_ref=buf.at[me], send_sem=ss, recv_sem=rs,
-                device_id=ids((me + d) % count), device_id_type=MESH,
+                device_id=ids(k + (me <= k).astype(jnp.int32)), device_id_type=MESH,
             ).start()
         others = buf.at[pl.ds(0, count - 1)]
 
@@ -498,7 +508,7 @@
     plane = n_gy * n_zz
     buf2[gy * n_zz + zz] = arrived1()
     arrived2, sent2 = exchange(
-        buf2, plane, gy * n_zz + zz, lambda k: {"gy": k // n_zz, "zz": k % n_zz}, ss2, rs2
+        buf2, plane, gy * n_zz + zz, lambda k: {"gy": lax.div(k, n_zz), "zz": lax.rem(k, n_zz)}, ss2, rs2
     )
 
     dn_x.wait_recv()

time: 33.5 us -> 33.4 us (level)
  no operation moved by 1% of the time
where the time goes in v6:
time: 33.4 us; the launch traced here: 33.3 us
  Pallas kernels  32.7 us (98%)
  between operations  0.64 us (2%)
    pallas_call x1, Pallas kernels, body(): pl.pallas_call(functools.partial(kernel, sizes), out_shape=(jax.ShapeDtyp...  30.9 us
    pallas_call x1, Pallas kernels, body(): pl.pallas_call(write_out, out_shape=tuple((jax.ShapeDtypeStruct(x.shape,...  1.8 us

profile of v6, /device:TPU:1, one launch (start us, length us, event | category | flops | bytes accessed | tf_op | source)
XLA Modules:
  0.0 33.3 jit_solution(6524081203207166028)
XLA Ops:
  0.6 30.9 %shard_map.94 = (f32[2,4,3,8,16,128]{5,4,3,2,1,0:T(8,128)S(1)}, f32[2,4,3,8,16,128]{5,4,3,2,1,0:T(8,128)S(1)}, f32[2,4,4]{2,1,0:T(4,128)S(1)}) custom-call(s32[6]{0:T(128)} %pml_hbm.1, f32[4]{0:T(128)} %eps_r_hbm.1, f32[4]{0:T(128)} %eps_l_hbm.1, f32[2,4,4]{2,1,0:T(4,128)} %coef_hbm.1, f32[2,4]{1,0:T(2,128)} %ritz_hbm.1, s32[8,16,128]{2,1,0:T(8,128)} %mat_hbm.1, ...), custom_call_target="tpu_custom_call" | custom-call | tf_op jit(solution)/shard_map/pallas_call | solution.py:618
  31.5 1.8 %shard_map.95 = (f32[2,4,3,8,16,128]{5,4,3,2,1,0:T(8,128)}, f32[2,4,3,8,16,128]{5,4,3,2,1,0:T(8,128)}, f32[2,4,4]{2,1,0:T(4,128)}) custom-call(f32[2,4,3,8,16,128]{5,4,3,2,1,0:T(8,128)S(1)} %get-tuple-element.6.basis, f32[2,4,3,8,16,128]{5,4,3,2,1,0:T(8,128)S(1)} %get-tuple-element.7.resid, f32[2,4,4]{2,1,0:T(4,128)S(1)} %get-tuple-element.8.gram), custom_call_target="tpu_custom_call" | custom-call | tf_op jit(solution)/shard_map/pallas_call | solution.py:661
